TPU v7x, 256 devices: a whole 4x4x8 slice. The times are simulated.
256 devices in a mesh: nodes: 64 (over x, z, core), feat: 4 (over y).
Axes of the slice: x: 4, y: 4, z: 8, core: 2. Of those that a mesh axis runs over, the one named last changes fastest.
Arguments:
- node_feats: bfloat16 [32768, 512], P('nodes', 'feat'), may hold values from -6 to 6
- weight_one: bfloat16 [512, 512], replicated, may hold values from -0.25 to 0.25
- weight_two: bfloat16 [512, 512], replicated, may hold values from -0.25 to 0.25
- adj_tiles: bfloat16 [256, 24, 128, 128], P('nodes'), may hold values from -0.109375 to 0.109375
- tile_owner: int32 [6144, 1], P('nodes'), may hold values from 0 to 63; in each aligned block of 96 rows (0 to 95, 96 to 191, ...) at most 2 rows name the same one
- tile_local: int32 [6144, 1], P('nodes'), may hold values from 0 to 3
- cotangent: bfloat16 [32768, 512], P('nodes', 'feat'), may hold values from -6 to 6
Outputs:
- layer_output: bfloat16 [32768, 512], P('nodes', 'feat')
- grad_one: float32 [512, 512], P('feat')
- grad_two: float32 [512, 512], P('feat')
Inputs may be any that keep to these rules, and one draw needn't show every extreme that they name: `tile_owner`: among the 96 tiles of one index of nodes, each owner index is named by at most 2 tiles, and exactly 2 for some owner.
All inputs are finite; a program needn't handle non-finite values.
Results may differ from a plain program's by a relative error of at most 0.0065.
Values may be sent and summed in bfloat16 or wider, within the bound.
No kernel may reach another device: no remote copies, remote signals or barrier semaphores. Data moves between devices by JAX's collectives and lax.ppermute only.
A program may use at most 128 MiB of HBM per device.

v0:
```python
import functools
import math

import jax
import jax.numpy as jnp
from jax import lax
from jax.experimental import pallas as pl
from jax.experimental.pallas import tpu as pltpu
from jax.sharding import PartitionSpec as P


NX, NZ, NC, NY = 4, 8, 2, 4


STRIDE = 32
UNROLL = 6
LATE = 8


def node_pairs(dx, dz, dc):
    pairs = []
    for x in range(NX):
        for z in range(NZ):
            for c in range(NC):
                there = (((x + dx) % NX) * NZ + (z + dz) % NZ) * NC + (c + dc) % NC
                pairs.append(((x * NZ + z) * NC + c, there))
    return pairs


def xor_pairs(bit):
    return [(i, i ^ bit) for i in range(NX * NZ * NC)]


def in_hbm(value):
    return pltpu.with_memory_space_constraint(value, pltpu.HBM)


def send(value, dx=0, dz=0, dc=0):
    return lax.ppermute(value, "nodes", node_pairs(dx, dz, dc))


def gather_y(value):
    pairs = [[(y, (y - r) % NY) for y in range(NY)] for r in range(NY)]
    return [value] + [lax.ppermute(value, "feat", pairs[r]) for r in range(1, NY)]


def ring_z(block):
    half = block.shape[0] // 2
    low, high = [block], [block]
    for _ in range(1, 4):
        low.append(send(low[-1], dz=1))
        high.append(send(high[-1], dz=-1))
    first = send(low[3][:half], dz=1)
    second = send(high[3][half:], dz=-1)
    return [block, high[1], high[2], high[3], (first, second), low[3], low[2], low[1]]


def gather_plane(own):
    nb = own.shape[0]
    beside = [send(own, dx=-r) for r in (1, 2, 3)]
    near, last = [], []
    for r, entry in enumerate(ring_z(join_call([own] + beside))):
        if r == NZ // 2:
            half = entry[0].shape[0]
            last = [(0, half, entry[0]), (half, half, entry[1])]
        else:
            near.append((r * NX * nb, NX * nb, entry))
    return near, last


def join_call(parts):
    size, blk, width = parts[0].shape
    n = len(parts)

    def kernel(*refs):
        for i in range(n):
            refs[n][i * size:(i + 1) * size] = refs[i][...]

    vmem = pl.BlockSpec(memory_space=pltpu.VMEM)
    return pl.pallas_call(
        kernel,
        out_shape=jax.ShapeDtypeStruct((n * size, blk, width), parts[0].dtype),
        in_specs=[vmem] * n,
        out_specs=vmem,
        compiler_params=pltpu.CompilerParams(vmem_limit_bytes=4 * 1024 * 1024),
        name="join",
    )(*parts)


def fold_kernel(p1, p3, up_far, down_far, up, down):
    half = up_far.shape[0]
    f32 = jnp.float32

    def one(i, carry):
        up[i] = (p1[i].astype(f32) + up_far[i].astype(f32)).astype(up.dtype)
        up[half + i] = p1[half + i]
        down[i] = p3[i]
        down[half + i] = (p3[half + i].astype(f32) + down_far[i].astype(f32)).astype(down.dtype)
        return carry

    lax.fori_loop(0, half, one, 0)


def fold_call(p1, p3, up_far, down_far):
    vmem = pl.BlockSpec(memory_space=pltpu.VMEM)
    return pl.pallas_call(
        fold_kernel,
        out_shape=[jax.ShapeDtypeStruct(p1.shape, p1.dtype)] * 2,
        in_specs=[vmem] * 4,
        out_specs=[vmem] * 2,
        compiler_params=pltpu.CompilerParams(vmem_limit_bytes=8 * 1024 * 1024),
        name="fold",
    )(p1, p3, up_far, down_far)


def sum_kernel(p0, up, down, keep, give):
    half = keep.shape[0]
    f32 = jnp.float32

    def one(i, carry):
        keep[i] = p0[i].astype(f32) + up[i].astype(f32) + down[i].astype(f32)
        far = half + i
        give[i] = (p0[far].astype(f32) + up[far].astype(f32) + down[far].astype(f32)).astype(give.dtype)
        return carry

    lax.fori_loop(0, half, one, 0)


def sum_call(p0, up, down):
    vmem = pl.BlockSpec(memory_space=pltpu.VMEM)
    size, width, blk = p0.shape
    return pl.pallas_call(
        sum_kernel,
        out_shape=[
            jax.ShapeDtypeStruct((size // 2, width, blk), jnp.float32),
            jax.ShapeDtypeStruct((size // 2, width, blk), p0.dtype),
        ],
        in_specs=[vmem] * 3,
        out_specs=[vmem] * 2,
        compiler_params=pltpu.CompilerParams(vmem_limit_bytes=8 * 1024 * 1024),
        name="sum",
    )(p0, up, down)


def reduce_plane(parts, nb):
    f32, bf = jnp.float32, jnp.bfloat16
    half = NZ * nb // 2
    far = parts[2]
    up_far = send(far[:half], dx=1)
    down_far = send(far[half:], dx=-1)
    up, down = fold_call(parts[1], parts[3], up_far, down_far)
    own, give = sum_call(parts[0], send(up, dx=1), send(down, dx=-1))
    own = own + lax.ppermute(give, "nodes", xor_pairs(NC)).astype(f32)
    for bit in (2, 4):
        half = own.shape[0] // 2
        give = own[half:].astype(bf)
        own = own[:half] + lax.ppermute(give, "nodes", xor_pairs(bit * NC)).astype(f32)
    return own


def halve(value, index):
    value, give = value
    value = value + lax.ppermute(give, "nodes", xor_pairs(1))
    for bit in (16,):
        half = value.shape[0] // 2
        upper = (index & bit) != 0
        mine = jnp.where(upper, value[half:], value[:half])
        give = jnp.where(upper, value[:half], value[half:])
        value = mine + lax.ppermute(give, "nodes", xor_pairs(bit))
    for bit in (32, 2, 4, 8):
        value = value + lax.ppermute(value, "nodes", xor_pairs(bit))
    return value


def double(value, index):
    for bit in (16, 1):
        upper = (index & bit) != 0
        other = lax.ppermute(value, "nodes", xor_pairs(bit))
        value = jnp.concatenate([jnp.where(upper, other, value), jnp.where(upper, value, other)], axis=0)
    return value


def plan_offsets(nb):
    span = 2 * nb * STRIDE
    counts = 4 * span
    late = counts + 4 * nb
    return span, counts, late, late + 8 * LATE * 3


def plan_kernel(place, col_a, col_b, lists, *, nb, per):
    bits = nb.bit_length() - 1
    x, z, c = place[0], place[1], place[2]
    total = NX * NZ * nb
    span, counts, late, _ = plan_offsets(nb)
    for j in range(4 * LATE):
        lists[late + j] = 0
        lists[late + 4 * LATE + j] = NX * nb
        lists[late + 8 * LATE + j] = 0
    for s, cols in enumerate((col_a, col_b)):

        def block(b, behind, cols=cols, s=s):
            base = (s * nb + b) * STRIDE

            def one(k, carry):
                early, every, behind = carry
                column = cols[b * per + k]
                local = column & (nb - 1)
                owner = column >> bits
                rx = ((owner >> 4) - x) & (NX - 1)
                zo = (owner >> 1) & (NZ - 1)
                rz = (zo - z) & (NZ - 1)
                rel = zo ^ z
                rank = ((rel & 1) << 2) | (rel & 2) | (rel >> 2)
                mine = jnp.where((owner & 1) == c, 1, 0)
                far = jnp.where(rz == NZ // 2, mine, 0)
                lists[base + early] = b * per + k
                lists[span + base + early] = (rz * NX + rx) * nb + local
                lists[2 * span + base + every] = b * per + k
                lists[3 * span + base + every] = (rx * NZ + rank) * nb + local
                at = late + 2 * LATE * s + behind
                lists[at] = b * per + k
                lists[at + 4 * LATE] = rx * nb + local
                lists[at + 8 * LATE] = b
                return early + mine - far, every + mine, behind + far

            early, every, behind = lax.fori_loop(0, per, one, (0, 0, behind))
            lists[counts + s * nb + b] = (early + UNROLL - 1) // UNROLL
            lists[counts + 2 * nb + s * nb + b] = (every + UNROLL - 1) // UNROLL
            for j in range(UNROLL):
                lists[base + early + j] = 0
                lists[span + base + early + j] = total
                lists[2 * span + base + every + j] = 0
                lists[3 * span + base + every + j] = total
            return behind

        behind = lax.fori_loop(0, nb, block, 0)
        at = late + 2 * LATE * s + behind
        lists[at] = 0
        lists[at + 4 * LATE] = NX * nb
        lists[at + 8 * LATE] = 0


def plan_call(place, col_a, col_b, nb, per):
    smem = pl.BlockSpec(memory_space=pltpu.SMEM)
    return pl.pallas_call(
        functools.partial(plan_kernel, nb=nb, per=per),
        out_shape=jax.ShapeDtypeStruct((plan_offsets(nb)[3],), jnp.int32),
        in_specs=[smem] * 3,
        out_specs=smem,
        name="plan",
    )(place, col_a, col_b)


def transposed_kernel(lists, tiles_a, tiles_b, cot_a, cot_b, *rest):
    outs, (acc, held_a, held_b, sems) = rest[:NX], rest[NX:]
    blk = held_a.shape[1]
    rows = cot_a.shape[0] // blk
    span, counts, _, _ = plan_offsets(rows)
    copy_a = pltpu.make_async_copy(tiles_a, held_a, sems.at[0])
    copy_b = pltpu.make_async_copy(tiles_b, held_b, sems.at[1])
    copy_a.start()
    copy_b.start()

    def clear(i, carry):
        acc[i] = jnp.zeros_like(acc[i])
        return carry

    lax.fori_loop(0, acc.shape[0], clear, 0)
    for s, (copy, tiles, cot) in enumerate(((copy_a, held_a, cot_a), (copy_b, held_b, cot_b))):
        copy.wait()

        def block(b, carry, s=s, tiles=tiles, cot=cot):
            turned = cot[pl.ds(pl.multiple_of(b * blk, blk), blk), :].T
            base = (s * rows + b) * STRIDE

            def one(i, carry):
                for j in range(UNROLL // 2):
                    at = base + i * UNROLL + 2 * j
                    one_tile, two_tile = lists[2 * span + at], lists[2 * span + at + 1]
                    right = jnp.concatenate([tiles[one_tile], tiles[two_tile]], axis=1)
                    term = jnp.dot(turned, right, preferred_element_type=jnp.float32)
                    one_slot, two_slot = lists[3 * span + at], lists[3 * span + at + 1]
                    acc[one_slot] = acc[one_slot] + term[:, :blk]
                    acc[two_slot] = acc[two_slot] + term[:, blk:]
                return carry

            return lax.fori_loop(0, lists[counts + 2 * rows + s * rows + b], one, carry)

        lax.fori_loop(0, rows, block, 0)
    size = outs[0].shape[0]

    def store(i, carry):
        for r, out in enumerate(outs):
            out[i] = acc[r * size + i].astype(out.dtype)
        return carry

    lax.fori_loop(0, size, store, 0)


def transposed_terms(lists, tiles_a, tiles_b, cot_a, cot_b, total):
    blk = tiles_a.shape[1]
    width = cot_a.shape[1]
    shape = jax.ShapeDtypeStruct((total // NX, width, blk), jnp.bfloat16)
    smem = pl.BlockSpec(memory_space=pltpu.SMEM)
    vmem = pl.BlockSpec(memory_space=pltpu.VMEM)
    free = pl.BlockSpec(memory_space=pltpu.HBM)
    return pl.pallas_call(
        transposed_kernel,
        out_shape=[shape] * NX,
        in_specs=[smem, free, free, vmem, vmem],
        out_specs=[vmem] * NX,
        scratch_shapes=[
            pltpu.VMEM((total + 1, width, blk), jnp.float32),
            pltpu.VMEM(tiles_a.shape, tiles_a.dtype),
            pltpu.VMEM(tiles_b.shape, tiles_b.dtype),
            pltpu.SemaphoreType.DMA((2,)),
        ],
        compiler_params=pltpu.CompilerParams(vmem_limit_bytes=32 * 1024 * 1024),
        name="transposed_terms",
    )(lists, in_hbm(tiles_a), in_hbm(tiles_b), cot_a, cot_b)


def early_call(lists, tiles_a, tiles_b, pieces, total, rows):
    blk = tiles_a.shape[1]
    width = pieces[0][2].shape[2]
    n = len(pieces)
    span, counts, _, _ = plan_offsets(rows)

    def kernel(lists, tiles_a, tiles_b, *rest):
        parts, (out_a, out_b, held, held_a, held_b, sems) = rest[:n], rest[n:]
        copies = [
            pltpu.make_async_copy(part.at[pl.ds(0, count)], held.at[pl.ds(at, count)], sems.at[i])
            for i, (part, (at, count, _)) in enumerate(zip(parts, pieces))
        ]
        copy_a = pltpu.make_async_copy(tiles_a, held_a, sems.at[n])
        copy_b = pltpu.make_async_copy(tiles_b, held_b, sems.at[n + 1])
        for copy in copies:
            copy.start()
        copy_b.start()
        copy_a.start()
        held[total] = jnp.zeros_like(held[total])
        for copy in copies:
            copy.wait()
        for s, copy, tiles, out in ((1, copy_b, held_b, out_b), (0, copy_a, held_a, out_a)):
            copy.wait()

            def block(b, carry, s=s, tiles=tiles, out=out):
                base = (s * rows + b) * STRIDE

                def one(i, summed):
                    for j in range(UNROLL // 2):
                        at = base + i * UNROLL + 2 * j
                        left = jnp.concatenate([tiles[lists[at]], tiles[lists[at + 1]]], axis=1)
                        one_slot, two_slot = lists[span + at], lists[span + at + 1]
                        right = jnp.concatenate([held[one_slot], held[two_slot]], axis=0)
                        summed = summed + jnp.dot(left, right, preferred_element_type=jnp.float32)
                    return summed

                zero = jnp.zeros((blk, width), jnp.float32)
                out[b] = lax.fori_loop(0, lists[counts + s * rows + b], one, zero)
                return carry

            lax.fori_loop(0, rows, block, 0)

    shape = jax.ShapeDtypeStruct((rows, blk, width), jnp.float32)
    smem = pl.BlockSpec(memory_space=pltpu.SMEM)
    vmem = pl.BlockSpec(memory_space=pltpu.VMEM)
    free = pl.BlockSpec(memory_space=pltpu.HBM)
    return pl.pallas_call(
        kernel,
        out_shape=[shape, shape],
        in_specs=[smem] + [free] * (n + 2),
        out_specs=[vmem, vmem],
        scratch_shapes=[
            pltpu.VMEM((total + 1, blk, width), jnp.bfloat16),
            pltpu.VMEM(tiles_a.shape, tiles_a.dtype),
            pltpu.VMEM(tiles_b.shape, tiles_b.dtype),
            pltpu.SemaphoreType.DMA((n + 2,)),
        ],
        compiler_params=pltpu.CompilerParams(vmem_limit_bytes=24 * 1024 * 1024),
        name="early",
    )(lists, in_hbm(tiles_a), in_hbm(tiles_b), *[in_hbm(part) for _, _, part in pieces])


def late_call(lists, tiles_a, tiles_b, last, early):
    rows, blk, width = early[0].shape
    n = len(last)
    zero = sum(count for _, count, _ in last)
    _, _, late, _ = plan_offsets(rows)

    def kernel(lists, tiles_a, tiles_b, early_a, early_b, *rest):
        parts, (out_a, out_b, held, got, sems) = rest[:n], rest[n:]
        copies = [
            pltpu.make_async_copy(part.at[pl.ds(0, count)], held.at[pl.ds(at, count)], sems.at[i])
            for i, (part, (at, count, _)) in enumerate(zip(parts, last))
        ]
        for s, tiles in ((0, tiles_a), (1, tiles_b)):
            for j in range(LATE):
                at = s * LATE + j
                tile = lists[late + 2 * LATE * s + j]
                copies.append(pltpu.make_async_copy(tiles.at[tile], got.at[at], sems.at[n + at]))
        for copy in copies:
            copy.start()
        held[zero] = jnp.zeros_like(held[zero])
        out_a[...] = early_a[...]
        out_b[...] = early_b[...]
        for copy in copies:
            copy.wait()
        for s, out in ((0, out_a), (1, out_b)):

            def some(i, carry, s=s, out=out):
                for j in range(2):
                    k = i * 2 + j
                    at = late + 2 * LATE * s + k
                    term = jnp.dot(got[s * LATE + k], held[lists[at + 4 * LATE]], preferred_element_type=jnp.float32)
                    row = lists[at + 8 * LATE]
                    out[row] = out[row] + term
                return carry

            lax.fori_loop(0, LATE // 2, some, 0)

    shape = jax.ShapeDtypeStruct((rows, blk, width), jnp.float32)
    smem = pl.BlockSpec(memory_space=pltpu.SMEM)
    vmem = pl.BlockSpec(memory_space=pltpu.VMEM)
    free = pl.BlockSpec(memory_space=pl.ANY)
    tiled = pl.BlockSpec(memory_space=pltpu.HBM)
    return pl.pallas_call(
        kernel,
        out_shape=[shape, shape],
        in_specs=[smem, tiled, tiled, vmem, vmem] + [free] * n,
        out_specs=[vmem, vmem],
        scratch_shapes=[
            pltpu.VMEM((zero + 1, blk, width), jnp.bfloat16),
            pltpu.VMEM((2 * LATE, blk, blk), tiles_a.dtype),
            pltpu.SemaphoreType.DMA((n + 2 * LATE,)),
        ],
        compiler_params=pltpu.CompilerParams(vmem_limit_bytes=8 * 1024 * 1024),
        name="late",
    )(lists, in_hbm(tiles_a), in_hbm(tiles_b), *early, *[part for _, _, part in last])


def mixing_kernel(place, p0, p1, p2, p3, w_in, w_out, z_out, own_out, mixed_out):
    y = place[3]
    nodes, width = p0.shape
    blk = mixed_out.shape[1]

    def block(b, carry):
        at = pl.ds(pl.multiple_of(b * blk, blk), blk)
        z = None
        for r, part in enumerate((p0, p1, p2, p3)):
            row = pl.multiple_of(((y + r) & (NY - 1)) * width, width)
            term = jnp.dot(part[at, :], w_in[pl.ds(row, width), :], preferred_element_type=jnp.float32)
            z = term if z is None else z + term
        z_out[at, :] = z
        hidden = (z * jax.nn.sigmoid(z)).astype(jnp.bfloat16)
        mixed_out[b] = jnp.dot(hidden, w_out[...], preferred_element_type=jnp.float32).astype(jnp.bfloat16)
        own = z_out[at, pl.ds(pl.multiple_of(y * width, width), width)]
        own_out[at, :] = (own * jax.nn.sigmoid(own)).astype(jnp.bfloat16)
        return carry

    lax.fori_loop(0, nodes // blk, block, 0)


def mixing_call(place, parts, w_in, w_out, nb):
    nodes, width = parts[0].shape
    full = w_in.shape[0]
    smem = pl.BlockSpec(memory_space=pltpu.SMEM)
    vmem = pl.BlockSpec(memory_space=pltpu.VMEM)
    return pl.pallas_call(
        mixing_kernel,
        out_shape=[
            jax.ShapeDtypeStruct((nodes, full), jnp.float32),
            jax.ShapeDtypeStruct((nodes, width), jnp.bfloat16),
            jax.ShapeDtypeStruct((nb, nodes // nb, width), jnp.bfloat16),
        ],
        in_specs=[smem] + [vmem] * (NY + 2),
        out_specs=[vmem] * 3,
        compiler_params=pltpu.CompilerParams(vmem_limit_bytes=16 * 1024 * 1024),
        name="mixing",
    )(place, *parts, w_in, w_out)


def grads_kernel(place, z_all, prop, own, q0, q1, q2, q3, w_two, keep, give, both, *, factor):
    y = place[3]
    nodes, width = prop.shape
    blk = 128 if nodes % 128 == 0 else nodes
    down = (((0,), (0,)), ((), ()))
    across = (((1,), (1,)), ((), ()))
    both[...] = jnp.zeros_like(both)

    def block(b, carry):
        at = pl.ds(pl.multiple_of(b * blk, blk), blk)
        hidden_grad = None
        for r, part in enumerate((q0, q1, q2, q3)):
            col = pl.multiple_of(((y + r) & (NY - 1)) * width, width)
            term = lax.dot_general(part[at, :], w_two[:, pl.ds(col, width)], across, preferred_element_type=jnp.float32)
            hidden_grad = term if hidden_grad is None else hidden_grad + term
            term = lax.dot_general(own[at, :], part[at, :], down, preferred_element_type=jnp.float32)
            both[1, :, pl.ds(col, width)] = both[1, :, pl.ds(col, width)] + term * factor
        z = z_all[at, :]
        sigma = jax.nn.sigmoid(z)
        grad_z = (hidden_grad * sigma * (1.0 + z * (1.0 - sigma))).astype(jnp.bfloat16)
        term = lax.dot_general(prop[at, :], grad_z, down, preferred_element_type=jnp.float32)
        both[0] = both[0] + term * factor
        return carry

    lax.fori_loop(0, nodes // blk, block, 0)
    mine = place[2]
    for r in range(NY):
        cols = slice(r * width, (r + 1) * width)
        rows = slice(r * width, (r + 1) * width)
        keep[rows, :] = both[mine, :, cols]
        give[rows, :] = both[1 - mine, :, cols]


def grads_call(place, z_all, prop, own, parts, w_two, factor):
    width = prop.shape[1]
    full = w_two.shape[0]
    smem = pl.BlockSpec(memory_space=pltpu.SMEM)
    vmem = pl.BlockSpec(memory_space=pltpu.VMEM)
    return pl.pallas_call(
        functools.partial(grads_kernel, factor=factor),
        out_shape=[jax.ShapeDtypeStruct((full, width), jnp.float32)] * 2,
        in_specs=[smem] + [vmem] * (NY + 4),
        out_specs=[vmem] * 2,
        scratch_shapes=[pltpu.VMEM((2, width, full), jnp.float32)],
        compiler_params=pltpu.CompilerParams(vmem_limit_bytes=16 * 1024 * 1024),
        name="grads",
    )(place, z_all, prop, own, *parts, w_two)


def step(node_feats, weight_one, weight_two, adj_tiles, tile_owner, tile_local, cotangent):
    nb, per, blk, _ = adj_tiles.shape
    nodes, width = node_feats.shape
    full = weight_one.shape[0]
    node_count = NX * NZ * NC
    index = lax.axis_index("nodes")
    y = lax.axis_index("feat")
    place = jnp.stack([index // (NZ * NC), (index // NC) % NZ, index % NC, y]).astype(jnp.int32)
    bf = jnp.bfloat16
    total = NX * NZ * nb

    tiles = adj_tiles.reshape(nb * per, blk, blk)
    column = (tile_owner * nb + tile_local)[:, 0]
    column_other = send(column, dc=1)
    tiles_other = send(tiles, dc=1)
    cot_other = send(cotangent, dc=1)
    lists = plan_call(place, column, column_other, nb, per)

    def spread(features):
        near, last = gather_plane(features)
        early = early_call(lists, tiles, tiles_other, near, total, nb)
        mine, theirs = late_call(lists, tiles, tiles_other, last, early)
        return (mine + send(theirs, dc=1)).reshape(nodes, width).astype(bf)

    terms = transposed_terms(lists, tiles, tiles_other, cotangent, cot_other, total)
    turned = jnp.swapaxes(reduce_plane(terms, nb), 1, 2).reshape(nodes, width).astype(bf)

    weight_out = lax.dynamic_slice_in_dim(weight_two, y * width, width, 1)
    prop_one = spread(node_feats.reshape(nb, blk, width))
    prop_parts = gather_y(prop_one)
    z_one, hidden_own, mixed = mixing_call(place, prop_parts, weight_one, weight_out, nb)

    turned_parts = gather_y(turned)
    factor = 1.0 / math.sqrt(nodes * node_count)
    both = grads_call(place, z_one, prop_one, hidden_own, turned_parts, weight_two, factor)
    part = halve(both, index)
    layer_output = spread(mixed)
    summed = double(part, index).reshape(2, NY, width, width)
    summed = jnp.swapaxes(summed, 1, 2).reshape(2, width, full)
    return (layer_output, summed[0], summed[1])


def solution(mesh):
    placed = (
        P("nodes", "feat"),
        P(),
        P(),
        P("nodes", None, None, None),
        P("nodes", None),
        P("nodes", None),
        P("nodes", "feat"),
    )
    return jax.shard_map(
        step,
        mesh=mesh,
        in_specs=placed,
        out_specs=(P("nodes", "feat"), P("feat", None), P("feat", None)),
        check_vma=False,
    )
```

profile of v0, /device:TPU:2, one launch (start us, length us, event | category | flops | bytes accessed | tf_op | source)
XLA Modules:
  0.0 216.3 jit_solution(11100201335983828775)
XLA Ops:
  1.2 0.7 add_bitcast_fusion.col_a
  2.6 4.2 %collective-permute-done.col_b = s32[96]{0:T(128)S(1)} collective-permute-done((s32[96]{0:T(128)S(1)}, s32[96]{0:T(128)S(1)}, u32[]{:S(2)}, u32[]{:S(2)}) %collective-permute-start) | collective-permute-done | bytes 416 | tf_op jit(solution)/shard_map/ppermute | solution.py:39
  7.3 5.9 %plan.1.lists = s32[1232]{0:T(1024)} custom-call(s32[4]{0:T(128)} %pad_add_fusion.place, s32[96]{0:T(128)} %copy-done.22, s32[96]{0:T(128)} %copy-done.23), custom_call_target="tpu_custom_call" | custom-call | tf_op jit(solution)/shard_map/plan/pallas_call | solution.py:245
  13.2 1.6 copy-done.9
  14.9 0.7 copy-done.4
  15.5 0.9 copy-done.6
  16.5 8.5 %transposed_terms.1 = (bf16[32,128,128]{2,1,0:T(8,128)(2,1)S(1)}, bf16[32,128,128]{2,1,0:T(8,128)(2,1)S(1)}, bf16[32,128,128]{2,1,0:T(8,128)(2,1)S(1)}, bf16[32,128,128]{2,1,0:T(8,128)(2,1)S(1)}) custom-call(s32[1232]{0:T(1024)S(1)} %copy-done.4, bf16[96,128,128]{2,1,0:T(8,128)(2,1)} %bitcast.38, bf16[96,128,128]{2,1,0:T(8,128)(2,1)} %copy-done.9, ...), custom_call_target="tpu_custom_call" | custom-call | tf_op jit(solution)/shard_map/transposed_terms/pallas_call | solution.py:307
  25.0 1.6 collective-permute-start.30
  26.6 0.8 collective-permute-start.31
  27.4 3.1 %collective-permute-start.2 = (bf16[4,128,128]{2,1,0:T(8,128)(2,1)S(1)}, bf16[4,128,128]{2,1,0:T(8,128)(2,1)S(1)}, u32[]{:S(2)}, u32[]{:S(2)}) collective-permute-start(bf16[4,128,128]{2,1,0:T(8,128)(2,1)S(1)} %bitcast.33), channel_id=1, source_target_pairs={{0,192},{4,196},{8,200},{12,204},{16,208},{20,212},{24,216},{28,22... | collective-permute-start | bytes 393224 | tf_op jit(solution)/shard_map/ppermute | solution.py:39
  30.6 1.5 collective-permute-start.4
  32.1 11.2 %collective-permute-done.2.refs_1_ = bf16[4,128,128]{2,1,0:T(8,128)(2,1)S(1)} collective-permute-done((bf16[4,128,128]{2,1,0:T(8,128)(2,1)S(1)}, bf16[4,128,128]{2,1,0:T(8,128)(2,1)S(1)}, u32[]{:S(2)}, u32[]{:S(2)}) %collective-permute-start.2) | collective-permute-done | bytes 131104 | tf_op jit(solution)/shard_map/ppermute | solution.py:39
  43.3 2.6 %collective-permute-done.3.refs_2_ = bf16[4,128,128]{2,1,0:T(8,128)(2,1)S(1)} collective-permute-done((bf16[4,128,128]{2,1,0:T(8,128)(2,1)S(1)}, bf16[4,128,128]{2,1,0:T(8,128)(2,1)S(1)}, u32[]{:S(2)}, u32[]{:S(2)}) %collective-permute-start.3) | collective-permute-done | bytes 131104 | tf_op jit(solution)/shard_map/ppermute | solution.py:39
  45.9 2.0 collective-permute-start.8
  47.9 3.6 %collective-permute-start.5 = (bf16[16,128,128]{2,1,0:T(8,128)(2,1)S(1)}, bf16[16,128,128]{2,1,0:T(8,128)(2,1)S(1)}, u32[]{:S(2)}, u32[]{:S(2)}) collective-permute-start(bf16[16,128,128]{2,1,0:T(8,128)(2,1)S(1)} %join.2.rest_0_), channel_id=1, source_target_pairs={{0,56},{4,60},{8,0},{12,4},{16,8},{20,12},{24,16},{28,20},{32,24},... | collective-permute-start | bytes 1572872 | tf_op jit(solution)/shard_map/ppermute | solution.py:39
  51.9 2.0 collective-permute-start.33
  53.9 7.4 %collective-permute-done.8.rest_6_ = bf16[16,128,128]{2,1,0:T(8,128)(2,1)S(1)} collective-permute-done((bf16[16,128,128]{2,1,0:T(8,128)(2,1)S(1)}, bf16[16,128,128]{2,1,0:T(8,128)(2,1)S(1)}, u32[]{:S(2)}, u32[]{:S(2)}) %collective-permute-start.8) | collective-permute-done | bytes 524320 | tf_op jit(solution)/shard_map/ppermute | solution.py:39
  61.3 3.2 %collective-permute-start.6 = (bf16[16,128,128]{2,1,0:T(8,128)(2,1)S(1)}, bf16[16,128,128]{2,1,0:T(8,128)(2,1)S(1)}, u32[]{:S(2)}, u32[]{:S(2)}) collective-permute-start(bf16[16,128,128]{2,1,0:T(8,128)(2,1)S(1)} %collective-permute-done.5.rest_1_), channel_id=1, source_target_pairs={{0,56},{4,60},{8,0},{12,4},{16,8},{20,12},{24,16},{28,20},{32,24},... | collective-permute-start | bytes 1572872 | tf_op jit(solution)/shard_map/ppermute | solution.py:39
  64.5 9.0 %collective-permute-done.9.rest_5_ = bf16[16,128,128]{2,1,0:T(8,128)(2,1)S(1)} collective-permute-done((bf16[16,128,128]{2,1,0:T(8,128)(2,1)S(1)}, bf16[16,128,128]{2,1,0:T(8,128)(2,1)S(1)}, u32[]{:S(2)}, u32[]{:S(2)}) %collective-permute-start.9) | collective-permute-done | bytes 524320 | tf_op jit(solution)/shard_map/ppermute | solution.py:39
  73.6 3.2 %collective-permute-start.7 = (bf16[16,128,128]{2,1,0:T(8,128)(2,1)S(1)}, bf16[16,128,128]{2,1,0:T(8,128)(2,1)S(1)}, u32[]{:S(2)}, u32[]{:S(2)}) collective-permute-start(bf16[16,128,128]{2,1,0:T(8,128)(2,1)S(1)} %collective-permute-done.6.rest_2_), channel_id=1, source_target_pairs={{0,56},{4,60},{8,0},{12,4},{16,8},{20,12},{24,16},{28,20},{32,24},... | collective-permute-start | bytes 1572872 | tf_op jit(solution)/shard_map/ppermute | solution.py:39
  77.4 8.5 %collective-permute-done.10.rest_4_ = bf16[16,128,128]{2,1,0:T(8,128)(2,1)S(1)} collective-permute-done((bf16[16,128,128]{2,1,0:T(8,128)(2,1)S(1)}, bf16[16,128,128]{2,1,0:T(8,128)(2,1)S(1)}, u32[]{:S(2)}, u32[]{:S(2)}) %collective-permute-start.10) | collective-permute-done | bytes 524320 | tf_op jit(solution)/shard_map/ppermute | solution.py:39
  85.9 2.6 %collective-permute-start.11 = (bf16[8,128,128]{2,1,0:T(8,128)(2,1)S(1)}, bf16[8,128,128]{2,1,0:T(8,128)(2,1)S(1)}, u32[]{:S(2)}, u32[]{:S(2)}) collective-permute-start(bf16[8,128,128]{2,1,0:T(8,128)(2,1)S(1)} %slice.62), channel_id=1, source_target_pairs={{0,8},{4,12},{8,16},{12,20},{16,24},{20,28},{24,32},{28,36},{32,40... | collective-permute-start | bytes 786440 | tf_op jit(solution)/shard_map/ppermute | solution.py:39
  88.7 1.9 collective-permute-start.12
  90.6 7.4 %early.2 = (f32[4,128,128]{2,1,0:T(8,128)S(1)}, f32[4,128,128]{2,1,0:T(8,128)S(1)}) custom-call(s32[1232]{0:T(1024)S(1)} %copy-done.4, bf16[96,128,128]{2,1,0:T(8,128)(2,1)} %bitcast.39, bf16[96,128,128]{2,1,0:T(8,128)(2,1)} %copy-done.9, bf16[16,128,128]{2,1,0:T(8,128)(2,1)} %copy-done.1, bf16[16,128,128]{2,1,0:T(8,128)(2,1)} %copy-done.19, ...), custom_call_target="tpu_custom_call" | custom-call | tf_op jit(solution)/shard_map/early/pallas_call | solution.py:369
  98.4 2.5 %collective-permute-done.12.rest_1_ = bf16[8,128,128]{2,1,0:T(8,128)(2,1)S(1)} collective-permute-done((bf16[8,128,128]{2,1,0:T(8,128)(2,1)S(1)}, bf16[8,128,128]{2,1,0:T(8,128)(2,1)S(1)}, u32[]{:S(2)}, u32[]{:S(2)}) %collective-permute-start.12) | collective-permute-done | bytes 262176 | tf_op jit(solution)/shard_map/ppermute | solution.py:39
  100.9 3.2 %late.2 = (f32[4,128,128]{2,1,0:T(8,128)S(1)}, f32[4,128,128]{2,1,0:T(8,128)S(1)}) custom-call(s32[1232]{0:T(1024)S(1)} %copy-done.4, bf16[96,128,128]{2,1,0:T(8,128)(2,1)} %bitcast.40, bf16[96,128,128]{2,1,0:T(8,128)(2,1)} %copy-done.9, f32[4,128,128]{2,1,0:T(8,128)S(1)} %get-tuple-element.24.early_a, f32[4,128,128]{2,1,0:T(8,128)S(1)} %get-tuple-element.25.early_b, ...), custom_call_target="tpu_custom_call" | custom-call | tf_op jit(solution)/shard_map/late/pallas_call | solution.py:427
  104.4 3.0 %collective-permute-start.35 = (bf16[8,128,128]{2,1,0:T(8,128)(2,1)S(1)}, bf16[8,128,128]{2,1,0:T(8,128)(2,1)S(1)}, u32[]{:S(2)}, u32[]{:S(2)}) collective-permute-start(bf16[8,128,128]{2,1,0:T(8,128)(2,1)S(1)} %slice.86), channel_id=1, source_target_pairs={{0,16},{4,20},{8,24},{12,28},{16,0},{20,4},{24,8},{28,12},{32,48},... | collective-permute-start | bytes 786440 | tf_op jit(solution)/shard_map/ppermute | solution.py:157
  107.4 3.1 %collective-permute-start.14 = (bf16[512,128]{1,0:T(8,128)(2,1)S(1)}, bf16[512,128]{1,0:T(8,128)(2,1)S(1)}, u32[]{:S(2)}, u32[]{:S(2)}) collective-permute-start(bf16[512,128]{1,0:T(8,128)(2,1)S(1)} %bitcast.24), channel_id=1, source_target_pairs={{0,3},{1,0},{2,1},{3,2},{4,7},{5,4},{6,5},{7,6},{8,11},{9,8},{10,9... | collective-permute-start | bytes 393224 | tf_op jit(solution)/shard_map/ppermute | solution.py:44
  110.5 0.6 collective-permute-start.15
  111.2 1.0 collective-permute-start.16
  112.2 4.3 %collective-permute-done.14.p1 = bf16[512,128]{1,0:T(8,128)(2,1)S(1)} collective-permute-done((bf16[512,128]{1,0:T(8,128)(2,1)S(1)}, bf16[512,128]{1,0:T(8,128)(2,1)S(1)}, u32[]{:S(2)}, u32[]{:S(2)}) %collective-permute-start.14) | collective-permute-done | bytes 131104 | tf_op jit(solution)/shard_map/ppermute | solution.py:44
  116.5 2.0 collective-permute-done.15.p2
  118.4 1.7 collective-permute-done.16.p3
  120.2 2.3 %mixing.1 = (f32[512,512]{1,0:T(8,128)S(1)}, bf16[512,128]{1,0:T(8,128)(2,1)S(1)}, bf16[4,128,128]{2,1,0:T(8,128)(2,1)S(1)}) custom-call(s32[4]{0:T(128)S(1)} %copy-done.8, bf16[512,128]{1,0:T(8,128)(2,1)S(1)} %bitcast.27, bf16[512,128]{1,0:T(8,128)(2,1)S(1)} %collective-permute-done.14.p1, bf16[512,128]{1,0:T(8,128)(2,1)S(1)} %collective-permute-done.15.p2, ...), custom_call_target="tpu_custom_call" | custom-call | tf_op jit(solution)/shard_map/mixing/pallas_call | solution.py:469
  122.5 2.7 %collective-permute-start.18 = (bf16[4,128,128]{2,1,0:T(8,128)(2,1)S(1)}, bf16[4,128,128]{2,1,0:T(8,128)(2,1)S(1)}, u32[]{:S(2)}, u32[]{:S(2)}) collective-permute-start(bf16[4,128,128]{2,1,0:T(8,128)(2,1)S(1)} %get-tuple-element.28.refs_0_), channel_id=1, source_target_pairs={{0,128},{4,132},{8,136},{12,140},{16,144},{20,148},{24,152},{28,15... | collective-permute-start | bytes 393224 | tf_op jit(solution)/shard_map/ppermute | solution.py:39
  125.3 1.1 slice_add_fusion
  126.4 3.7 %collective-permute-start.36 = (bf16[4,128,128]{2,1,0:T(8,128)(2,1)S(1)}, bf16[4,128,128]{2,1,0:T(8,128)(2,1)S(1)}, u32[]{:S(2)}, u32[]{:S(2)}) collective-permute-start(bf16[4,128,128]{2,1,0:T(8,128)(2,1)S(1)} %slice.87), channel_id=1, source_target_pairs={{0,32},{4,36},{8,40},{12,44},{16,48},{20,52},{24,56},{28,60},{32,0... | collective-permute-start | bytes 393224 | tf_op jit(solution)/shard_map/ppermute | solution.py:157
  130.1 1.4 collective-permute-done.18.refs_2_
  131.5 1.1 collective-permute-done.19.refs_3_
  132.9 1.8 collective-permute-start.23
  134.8 1.4 collective-permute-done.36
  136.4 2.6 %collective-permute-start.37 = (bf16[512,128]{1,0:T(8,128)(2,1)S(1)}, bf16[512,128]{1,0:T(8,128)(2,1)S(1)}, u32[]{:S(2)}, u32[]{:S(2)}) collective-permute-start(bf16[512,128]{1,0:T(8,128)(2,1)S(1)} %bitcast.29), channel_id=1, source_target_pairs={{0,3},{1,0},{2,1},{3,2},{4,7},{5,4},{6,5},{7,6},{8,11},{9,8},{10,9... | collective-permute-start | bytes 393224 | tf_op jit(solution)/shard_map/ppermute | solution.py:44
  139.0 0.6 collective-permute-start.38
  140.1 2.8 %collective-permute-done.37.q1 = bf16[512,128]{1,0:T(8,128)(2,1)S(1)} collective-permute-done((bf16[512,128]{1,0:T(8,128)(2,1)S(1)}, bf16[512,128]{1,0:T(8,128)(2,1)S(1)}, u32[]{:S(2)}, u32[]{:S(2)}) %collective-permute-start.37) | collective-permute-done | bytes 131104 | tf_op jit(solution)/shard_map/ppermute | solution.py:44
  142.9 2.6 %collective-permute-done.38.q2 = bf16[512,128]{1,0:T(8,128)(2,1)S(1)} collective-permute-done((bf16[512,128]{1,0:T(8,128)(2,1)S(1)}, bf16[512,128]{1,0:T(8,128)(2,1)S(1)}, u32[]{:S(2)}, u32[]{:S(2)}) %collective-permute-start.38) | collective-permute-done | bytes 131104 | tf_op jit(solution)/shard_map/ppermute | solution.py:44
  145.6 1.3 collective-permute-done.39.q3
  146.9 2.8 %grads.1 = (f32[512,128]{1,0:T(8,128)S(1)}, f32[512,128]{1,0:T(8,128)S(1)}) custom-call(s32[4]{0:T(128)S(1)} %copy-done.8, f32[512,512]{1,0:T(8,128)S(1)} %get-tuple-element.33.z_all, bf16[512,128]{1,0:T(8,128)(2,1)S(1)} %bitcast.28, bf16[512,128]{1,0:T(8,128)(2,1)S(1)} %get-tuple-element.34.own, bf16[512,128]{1,0:T(8,128)(2,1)S(1)} %bitcast.32, ...), custom_call_target="tpu_custom_call" | custom-call | tf_op jit(solution)/shard_map/grads/pallas_call | solution.py:521
  149.8 2.2 collective-permute-start.21
  152.0 2.8 %collective-permute-start.41 = (f32[256,128]{1,0:T(8,128)S(1)}, f32[256,128]{1,0:T(8,128)S(1)}, u32[]{:S(2)}, u32[]{:S(2)}) collective-permute-start(f32[256,128]{1,0:T(8,128)S(1)} %slice_select_fusion), channel_id=1, source_target_pairs={{0,64},{4,68},{8,72},{12,76},{16,80},{20,84},{24,88},{28,92},{32,9... | collective-permute-start | bytes 393224 | tf_op jit(solution)/shard_map/ppermute | solution.py:169
  154.9 9.2 %collective-permute-done.21.rest_2_ = bf16[16,128,128]{2,1,0:T(8,128)(2,1)S(1)} collective-permute-done((bf16[16,128,128]{2,1,0:T(8,128)(2,1)S(1)}, bf16[16,128,128]{2,1,0:T(8,128)(2,1)S(1)}, u32[]{:S(2)}, u32[]{:S(2)}) %collective-permute-start.21) | collective-permute-done | bytes 524320 | tf_op jit(solution)/shard_map/ppermute | solution.py:39
  164.1 3.3 %collective-permute-start.22 = (bf16[16,128,128]{2,1,0:T(8,128)(2,1)S(1)}, bf16[16,128,128]{2,1,0:T(8,128)(2,1)S(1)}, u32[]{:S(2)}, u32[]{:S(2)}) collective-permute-start(bf16[16,128,128]{2,1,0:T(8,128)(2,1)S(1)} %collective-permute-done.21.rest_2_), channel_id=1, source_target_pairs={{0,56},{4,60},{8,0},{12,4},{16,8},{20,12},{24,16},{28,20},{32,24},... | collective-permute-start | bytes 1572872 | tf_op jit(solution)/shard_map/ppermute | solution.py:39
  167.5 3.1 %collective-permute-start.42 = (f32[256,128]{1,0:T(8,128)S(1)}, f32[256,128]{1,0:T(8,128)S(1)}, u32[]{:S(2)}, u32[]{:S(2)}) collective-permute-start(f32[256,128]{1,0:T(8,128)S(1)} %select_add_fusion), channel_id=1, source_target_pairs={{0,128},{4,132},{8,136},{12,140},{16,144},{20,148},{24,152},{28,15... | collective-permute-start | bytes 393224 | tf_op jit(solution)/shard_map/ppermute | solution.py:171
  170.5 3.5 %collective-permute-done.42 = f32[256,128]{1,0:T(8,128)S(1)} collective-permute-done((f32[256,128]{1,0:T(8,128)S(1)}, f32[256,128]{1,0:T(8,128)S(1)}, u32[]{:S(2)}, u32[]{:S(2)}) %collective-permute-start.42) | collective-permute-done | bytes 131104 | tf_op jit(solution)/shard_map/ppermute | solution.py:171
  174.1 7.6 %collective-permute-done.43 = f32[256,128]{1,0:T(8,128)S(1)} collective-permute-done((f32[256,128]{1,0:T(8,128)S(1)}, f32[256,128]{1,0:T(8,128)S(1)}, u32[]{:S(2)}, u32[]{:S(2)}) %collective-permute-start.43) | collective-permute-done | bytes 131104 | tf_op jit(solution)/shard_map/ppermute | solution.py:171
  181.9 2.6 %collective-permute-start.26 = (bf16[8,128,128]{2,1,0:T(8,128)(2,1)S(1)}, bf16[8,128,128]{2,1,0:T(8,128)(2,1)S(1)}, u32[]{:S(2)}, u32[]{:S(2)}) collective-permute-start(bf16[8,128,128]{2,1,0:T(8,128)(2,1)S(1)} %slice.64), channel_id=1, source_target_pairs={{0,8},{4,12},{8,16},{12,20},{16,24},{20,28},{24,32},{28,36},{32,40... | collective-permute-start | bytes 786440 | tf_op jit(solution)/shard_map/ppermute | solution.py:39
  184.5 0.8 collective-permute-start.27
  185.3 5.7 %collective-permute-done.44 = f32[256,128]{1,0:T(8,128)S(1)} collective-permute-done((f32[256,128]{1,0:T(8,128)S(1)}, f32[256,128]{1,0:T(8,128)S(1)}, u32[]{:S(2)}, u32[]{:S(2)}) %collective-permute-start.44) | collective-permute-done | bytes 131104 | tf_op jit(solution)/shard_map/ppermute | solution.py:171
  191.0 2.2 %collective-permute-start.45 = (f32[256,128]{1,0:T(8,128)S(1)}, f32[256,128]{1,0:T(8,128)S(1)}, u32[]{:S(2)}, u32[]{:S(2)}) collective-permute-start(f32[256,128]{1,0:T(8,128)S(1)} %add.61), channel_id=1, source_target_pairs={{0,32},{4,36},{8,40},{12,44},{16,48},{20,52},{24,56},{28,60},{32,0... | collective-permute-start | bytes 393224 | tf_op jit(solution)/shard_map/ppermute | solution.py:171
  193.2 8.4 %collective-permute-done.45 = f32[256,128]{1,0:T(8,128)S(1)} collective-permute-done((f32[256,128]{1,0:T(8,128)S(1)}, f32[256,128]{1,0:T(8,128)S(1)}, u32[]{:S(2)}, u32[]{:S(2)}) %collective-permute-start.45) | collective-permute-done | bytes 131104 | tf_op jit(solution)/shard_map/ppermute | solution.py:171
  202.0 7.4 %early.3 = (f32[4,128,128]{2,1,0:T(8,128)S(1)}, f32[4,128,128]{2,1,0:T(8,128)S(1)}) custom-call(s32[1232]{0:T(1024)S(1)} %copy-done.5, bf16[96,128,128]{2,1,0:T(8,128)(2,1)} %bitcast.41, bf16[96,128,128]{2,1,0:T(8,128)(2,1)} %copy-done.9, bf16[16,128,128]{2,1,0:T(8,128)(2,1)} %copy-done, bf16[16,128,128]{2,1,0:T(8,128)(2,1)} %copy-done.15, ...), custom_call_target="tpu_custom_call" | custom-call | tf_op jit(solution)/shard_map/early/pallas_call | solution.py:369
  209.5 3.2 %late.3 = (f32[4,128,128]{2,1,0:T(8,128)S(1)}, f32[4,128,128]{2,1,0:T(8,128)S(1)}) custom-call(s32[1232]{0:T(1024)S(1)} %copy-done.5, bf16[96,128,128]{2,1,0:T(8,128)(2,1)} %bitcast.42, bf16[96,128,128]{2,1,0:T(8,128)(2,1)} %copy-done.9, f32[4,128,128]{2,1,0:T(8,128)S(1)} %get-tuple-element.29.early_a, f32[4,128,128]{2,1,0:T(8,128)S(1)} %get-tuple-element.30.early_b, ...), custom_call_target="tpu_custom_call" | custom-call | tf_op jit(solution)/shard_map/late/pallas_call | solution.py:427
  213.4 0.9 collective-permute-done.28
  214.3 0.7 add_convert_fusion
  215.4 0.8 copy_bitcast_fusion
  (123 shorter events, 7.0 us)
Async XLA Ops:
  0.6 12.6 %collective-permute-start.1 = (bf16[96,128,128]{2,1,0:T(8,128)(2,1)}, bf16[96,128,128]{2,1,0:T(8,128)(2,1)S(1)}, u32[]{:S(2)}, u32[]{:S(2)}) collective-permute-start(bf16[96,128,128]{2,1,0:T(8,128)(2,1)} %bitcast.37), channel_id=1, source_target_pairs={{0,4},{4,0},{8,12},{12,8},{16,20},{20,16},{24,28},{28,24},{32,36},... | collective-permute-start | bytes 9437192 | tf_op jit(solution)/shard_map/ppermute | solution.py:39
  0.7 12.5 %collective-permute-start.29 = (bf16[512,128]{1,0:T(8,128)(2,1)}, bf16[512,128]{1,0:T(8,128)(2,1)S(1)}, u32[]{:S(2)}, u32[]{:S(2)}) collective-permute-start(bf16[512,128]{1,0:T(8,128)(2,1)} %cot_a.1), channel_id=1, source_target_pairs={{0,4},{4,0},{8,12},{12,8},{16,20},{20,16},{24,28},{28,24},{32,36},... | collective-permute-start | bytes 393224 | tf_op jit(solution)/shard_map/ppermute | solution.py:39
  1.9 4.9 %collective-permute-start = (s32[96]{0:T(128)S(1)}, s32[96]{0:T(128)S(1)}, u32[]{:S(2)}, u32[]{:S(2)}) collective-permute-start(s32[96]{0:T(128)S(1)} %add_bitcast_fusion.col_a), channel_id=1, source_target_pairs={{0,4},{4,0},{8,12},{12,8},{16,20},{20,16},{24,28},{28,24},{32,36},... | collective-permute-start | bytes 1160 | tf_op jit(solution)/shard_map/ppermute | solution.py:39
  16.5 11.0 %copy-start.7 = (bf16[512,128]{1,0:T(8,128)(2,1)S(1)}, bf16[512,128]{1,0:T(8,128)(2,1)}, u32[]{:S(2)}) copy-start(bf16[512,128]{1,0:T(8,128)(2,1)} %param.7) | copy-start | bytes 393220
  25.0 26.5 %collective-permute-start.30 = (bf16[16,128,128]{2,1,0:T(8,128)(2,1)S(1)}, bf16[16,128,128]{2,1,0:T(8,128)(2,1)S(1)}, u32[]{:S(2)}, u32[]{:S(2)}) collective-permute-start(bf16[16,128,128]{2,1,0:T(8,128)(2,1)S(1)} %get-tuple-element.46), channel_id=1, source_target_pairs={{0,64},{4,68},{8,72},{12,76},{16,80},{20,84},{24,88},{28,92},{32,9... | collective-permute-start | bytes 1572872 | tf_op jit(solution)/shard_map/ppermute | solution.py:39
  26.6 24.9 %collective-permute-start.31 = (bf16[16,128,128]{2,1,0:T(8,128)(2,1)S(1)}, bf16[16,128,128]{2,1,0:T(8,128)(2,1)S(1)}, u32[]{:S(2)}, u32[]{:S(2)}) collective-permute-start(bf16[16,128,128]{2,1,0:T(8,128)(2,1)S(1)} %get-tuple-element.45), channel_id=1, source_target_pairs={{0,192},{4,196},{8,200},{12,204},{16,208},{20,212},{24,216},{28,22... | collective-permute-start | bytes 1572872 | tf_op jit(solution)/shard_map/ppermute | solution.py:39
  27.4 15.9 %collective-permute-start.2 = (bf16[4,128,128]{2,1,0:T(8,128)(2,1)S(1)}, bf16[4,128,128]{2,1,0:T(8,128)(2,1)S(1)}, u32[]{:S(2)}, u32[]{:S(2)}) collective-permute-start(bf16[4,128,128]{2,1,0:T(8,128)(2,1)S(1)} %bitcast.33), channel_id=1, source_target_pairs={{0,192},{4,196},{8,200},{12,204},{16,208},{20,212},{24,216},{28,22... | collective-permute-start | bytes 393224 | tf_op jit(solution)/shard_map/ppermute | solution.py:39
  30.6 15.3 %collective-permute-start.3 = (bf16[4,128,128]{2,1,0:T(8,128)(2,1)S(1)}, bf16[4,128,128]{2,1,0:T(8,128)(2,1)S(1)}, u32[]{:S(2)}, u32[]{:S(2)}) collective-permute-start(bf16[4,128,128]{2,1,0:T(8,128)(2,1)S(1)} %bitcast.34), channel_id=1, source_target_pairs={{0,128},{4,132},{8,136},{12,140},{16,144},{20,148},{24,152},{28,15... | collective-permute-start | bytes 393224 | tf_op jit(solution)/shard_map/ppermute | solution.py:39
  30.6 15.3 %collective-permute-start.4 = (bf16[4,128,128]{2,1,0:T(8,128)(2,1)S(1)}, bf16[4,128,128]{2,1,0:T(8,128)(2,1)S(1)}, u32[]{:S(2)}, u32[]{:S(2)}) collective-permute-start(bf16[4,128,128]{2,1,0:T(8,128)(2,1)S(1)} %bitcast.35), channel_id=1, source_target_pairs={{0,64},{4,68},{8,72},{12,76},{16,80},{20,84},{24,88},{28,92},{32,9... | collective-permute-start | bytes 393224 | tf_op jit(solution)/shard_map/ppermute | solution.py:39
  45.9 31.4 %copy-start.1 = (bf16[16,128,128]{2,1,0:T(8,128)(2,1)}, bf16[16,128,128]{2,1,0:T(8,128)(2,1)S(1)}, u32[]{:S(2)}) copy-start(bf16[16,128,128]{2,1,0:T(8,128)(2,1)S(1)} %join.2.rest_0_) | copy-start | bytes 1572868
  45.9 15.4 %collective-permute-start.8 = (bf16[16,128,128]{2,1,0:T(8,128)(2,1)S(1)}, bf16[16,128,128]{2,1,0:T(8,128)(2,1)S(1)}, u32[]{:S(2)}, u32[]{:S(2)}) collective-permute-start(bf16[16,128,128]{2,1,0:T(8,128)(2,1)S(1)} %join.2.rest_0_), channel_id=1, source_target_pairs={{0,8},{4,12},{8,16},{12,20},{16,24},{20,28},{24,32},{28,36},{32,40... | collective-permute-start | bytes 1572872 | tf_op jit(solution)/shard_map/ppermute | solution.py:39
  47.9 13.4 %collective-permute-start.5 = (bf16[16,128,128]{2,1,0:T(8,128)(2,1)S(1)}, bf16[16,128,128]{2,1,0:T(8,128)(2,1)S(1)}, u32[]{:S(2)}, u32[]{:S(2)}) collective-permute-start(bf16[16,128,128]{2,1,0:T(8,128)(2,1)S(1)} %join.2.rest_0_), channel_id=1, source_target_pairs={{0,56},{4,60},{8,0},{12,4},{16,8},{20,12},{24,16},{28,20},{32,24},... | collective-permute-start | bytes 1572872 | tf_op jit(solution)/shard_map/ppermute | solution.py:39
  51.8 25.0 %collective-permute-start.32 = (bf16[32,128,128]{2,1,0:T(8,128)(2,1)S(1)}, bf16[32,128,128]{2,1,0:T(8,128)(2,1)S(1)}, u32[]{:S(2)}, u32[]{:S(2)}) collective-permute-start(bf16[32,128,128]{2,1,0:T(8,128)(2,1)S(1)} %get-tuple-element.39), channel_id=1, source_target_pairs={{0,64},{4,68},{8,72},{12,76},{16,80},{20,84},{24,88},{28,92},{32,9... | collective-permute-start | bytes 3145736 | tf_op jit(solution)/shard_map/ppermute | solution.py:39
  51.9 24.9 %collective-permute-start.33 = (bf16[32,128,128]{2,1,0:T(8,128)(2,1)S(1)}, bf16[32,128,128]{2,1,0:T(8,128)(2,1)S(1)}, u32[]{:S(2)}, u32[]{:S(2)}) collective-permute-start(bf16[32,128,128]{2,1,0:T(8,128)(2,1)S(1)} %get-tuple-element.40), channel_id=1, source_target_pairs={{0,192},{4,196},{8,200},{12,204},{16,208},{20,212},{24,216},{28,22... | collective-permute-start | bytes 3145736 | tf_op jit(solution)/shard_map/ppermute | solution.py:39
  61.3 29.3 %copy-start.18 = (bf16[16,128,128]{2,1,0:T(8,128)(2,1)}, bf16[16,128,128]{2,1,0:T(8,128)(2,1)S(1)}, u32[]{:S(2)}) copy-start(bf16[16,128,128]{2,1,0:T(8,128)(2,1)S(1)} %collective-permute-done.8.rest_6_) | copy-start | bytes 1572868
  61.3 12.3 %collective-permute-start.9 = (bf16[16,128,128]{2,1,0:T(8,128)(2,1)S(1)}, bf16[16,128,128]{2,1,0:T(8,128)(2,1)S(1)}, u32[]{:S(2)}, u32[]{:S(2)}) collective-permute-start(bf16[16,128,128]{2,1,0:T(8,128)(2,1)S(1)} %collective-permute-done.8.rest_6_), channel_id=1, source_target_pairs={{0,8},{4,12},{8,16},{12,20},{16,24},{20,28},{24,32},{28,36},{32,40... | collective-permute-start | bytes 1572872 | tf_op jit(solution)/shard_map/ppermute | solution.py:39
  61.3 29.3 %copy-start.19 = (bf16[16,128,128]{2,1,0:T(8,128)(2,1)}, bf16[16,128,128]{2,1,0:T(8,128)(2,1)S(1)}, u32[]{:S(2)}) copy-start(bf16[16,128,128]{2,1,0:T(8,128)(2,1)S(1)} %collective-permute-done.5.rest_1_) | copy-start | bytes 1572868
  61.3 12.3 %collective-permute-start.6 = (bf16[16,128,128]{2,1,0:T(8,128)(2,1)S(1)}, bf16[16,128,128]{2,1,0:T(8,128)(2,1)S(1)}, u32[]{:S(2)}, u32[]{:S(2)}) collective-permute-start(bf16[16,128,128]{2,1,0:T(8,128)(2,1)S(1)} %collective-permute-done.5.rest_1_), channel_id=1, source_target_pairs={{0,56},{4,60},{8,0},{12,4},{16,8},{20,12},{24,16},{28,20},{32,24},... | collective-permute-start | bytes 1572872 | tf_op jit(solution)/shard_map/ppermute | solution.py:39
  73.6 17.0 %copy-start.20 = (bf16[16,128,128]{2,1,0:T(8,128)(2,1)}, bf16[16,128,128]{2,1,0:T(8,128)(2,1)S(1)}, u32[]{:S(2)}) copy-start(bf16[16,128,128]{2,1,0:T(8,128)(2,1)S(1)} %collective-permute-done.9.rest_5_) | copy-start | bytes 1572868
  73.6 12.3 %collective-permute-start.10 = (bf16[16,128,128]{2,1,0:T(8,128)(2,1)S(1)}, bf16[16,128,128]{2,1,0:T(8,128)(2,1)S(1)}, u32[]{:S(2)}, u32[]{:S(2)}) collective-permute-start(bf16[16,128,128]{2,1,0:T(8,128)(2,1)S(1)} %collective-permute-done.9.rest_5_), channel_id=1, source_target_pairs={{0,8},{4,12},{8,16},{12,20},{16,24},{20,28},{24,32},{28,36},{32,40... | collective-permute-start | bytes 1572872 | tf_op jit(solution)/shard_map/ppermute | solution.py:39
  73.6 17.0 %copy-start.21 = (bf16[16,128,128]{2,1,0:T(8,128)(2,1)}, bf16[16,128,128]{2,1,0:T(8,128)(2,1)S(1)}, u32[]{:S(2)}) copy-start(bf16[16,128,128]{2,1,0:T(8,128)(2,1)S(1)} %collective-permute-done.6.rest_2_) | copy-start | bytes 1572868
  73.6 15.1 %collective-permute-start.7 = (bf16[16,128,128]{2,1,0:T(8,128)(2,1)S(1)}, bf16[16,128,128]{2,1,0:T(8,128)(2,1)S(1)}, u32[]{:S(2)}, u32[]{:S(2)}) collective-permute-start(bf16[16,128,128]{2,1,0:T(8,128)(2,1)S(1)} %collective-permute-done.6.rest_2_), channel_id=1, source_target_pairs={{0,56},{4,60},{8,0},{12,4},{16,8},{20,12},{24,16},{28,20},{32,24},... | collective-permute-start | bytes 1572872 | tf_op jit(solution)/shard_map/ppermute | solution.py:39
  77.3 26.9 %collective-permute-start.34 = (bf16[16,128,128]{2,1,0:T(8,128)(2,1)S(1)}, bf16[16,128,128]{2,1,0:T(8,128)(2,1)S(1)}, u32[]{:S(2)}, u32[]{:S(2)}) collective-permute-start(bf16[16,128,128]{2,1,0:T(8,128)(2,1)S(1)} %get-tuple-element.42), channel_id=1, source_target_pairs={{0,8},{4,12},{8,0},{12,4},{16,24},{20,28},{24,16},{28,20},{32,40},... | collective-permute-start | bytes 1572872 | tf_op jit(solution)/shard_map/ppermute | solution.py:153
  85.9 12.5 %collective-permute-start.11 = (bf16[8,128,128]{2,1,0:T(8,128)(2,1)S(1)}, bf16[8,128,128]{2,1,0:T(8,128)(2,1)S(1)}, u32[]{:S(2)}, u32[]{:S(2)}) collective-permute-start(bf16[8,128,128]{2,1,0:T(8,128)(2,1)S(1)} %slice.62), channel_id=1, source_target_pairs={{0,8},{4,12},{8,16},{12,20},{16,24},{20,28},{24,32},{28,36},{32,40... | collective-permute-start | bytes 786440 | tf_op jit(solution)/shard_map/ppermute | solution.py:39
  88.7 12.2 %collective-permute-start.12 = (bf16[8,128,128]{2,1,0:T(8,128)(2,1)S(1)}, bf16[8,128,128]{2,1,0:T(8,128)(2,1)S(1)}, u32[]{:S(2)}, u32[]{:S(2)}) collective-permute-start(bf16[8,128,128]{2,1,0:T(8,128)(2,1)S(1)} %slice.63), channel_id=1, source_target_pairs={{0,56},{4,60},{8,0},{12,4},{16,8},{20,12},{24,16},{28,20},{32,24},... | collective-permute-start | bytes 786440 | tf_op jit(solution)/shard_map/ppermute | solution.py:39
  104.1 8.0 %copy-start.2 = (bf16[512,512]{1,0:T(8,128)(2,1)S(1)}, bf16[512,512]{1,0:T(8,128)(2,1)}, u32[]{:S(2)}) copy-start(bf16[512,512]{1,0:T(8,128)(2,1)} %w_two.1) | copy-start | bytes 1572868
  104.1 16.1 %copy-start.3 = (bf16[512,512]{1,0:T(8,128)(2,1)S(1)}, bf16[512,512]{1,0:T(8,128)(2,1)}, u32[]{:S(2)}) copy-start(bf16[512,512]{1,0:T(8,128)(2,1)} %w_in.1) | copy-start | bytes 1572868
  104.1 16.1 %copy-start.8 = (s32[4]{0:T(128)S(1)}, s32[4]{0:T(128)}, u32[]{:S(2)}) copy-start(s32[4]{0:T(128)} %pad_add_fusion.place) | copy-start | bytes 52
  104.1 3.3 %collective-permute-start.13 = (f32[4,128,128]{2,1,0:T(8,128)S(1)}, f32[4,128,128]{2,1,0:T(8,128)S(1)}, u32[]{:S(2)}, u32[]{:S(2)}) collective-permute-start(f32[4,128,128]{2,1,0:T(8,128)S(1)} %get-tuple-element.27), channel_id=1, source_target_pairs={{0,4},{4,0},{8,12},{12,8},{16,20},{20,16},{24,28},{28,24},{32,36},... | collective-permute-start | bytes 786440 | tf_op jit(solution)/shard_map/ppermute | solution.py:39
  104.4 20.8 %collective-permute-start.35 = (bf16[8,128,128]{2,1,0:T(8,128)(2,1)S(1)}, bf16[8,128,128]{2,1,0:T(8,128)(2,1)S(1)}, u32[]{:S(2)}, u32[]{:S(2)}) collective-permute-start(bf16[8,128,128]{2,1,0:T(8,128)(2,1)S(1)} %slice.86), channel_id=1, source_target_pairs={{0,16},{4,20},{8,24},{12,28},{16,0},{20,4},{24,8},{28,12},{32,48},... | collective-permute-start | bytes 786440 | tf_op jit(solution)/shard_map/ppermute | solution.py:157
  107.4 9.0 %collective-permute-start.14 = (bf16[512,128]{1,0:T(8,128)(2,1)S(1)}, bf16[512,128]{1,0:T(8,128)(2,1)S(1)}, u32[]{:S(2)}, u32[]{:S(2)}) collective-permute-start(bf16[512,128]{1,0:T(8,128)(2,1)S(1)} %bitcast.24), channel_id=1, source_target_pairs={{0,3},{1,0},{2,1},{3,2},{4,7},{5,4},{6,5},{7,6},{8,11},{9,8},{10,9... | collective-permute-start | bytes 393224 | tf_op jit(solution)/shard_map/ppermute | solution.py:44
  110.5 7.9 %collective-permute-start.15 = (bf16[512,128]{1,0:T(8,128)(2,1)S(1)}, bf16[512,128]{1,0:T(8,128)(2,1)S(1)}, u32[]{:S(2)}, u32[]{:S(2)}) collective-permute-start(bf16[512,128]{1,0:T(8,128)(2,1)S(1)} %bitcast.25), channel_id=1, source_target_pairs={{0,2},{1,3},{2,0},{3,1},{4,6},{5,7},{6,4},{7,5},{8,10},{9,11},{10,... | collective-permute-start | bytes 393224 | tf_op jit(solution)/shard_map/ppermute | solution.py:44
  111.2 9.0 %collective-permute-start.16 = (bf16[512,128]{1,0:T(8,128)(2,1)S(1)}, bf16[512,128]{1,0:T(8,128)(2,1)S(1)}, u32[]{:S(2)}, u32[]{:S(2)}) collective-permute-start(bf16[512,128]{1,0:T(8,128)(2,1)S(1)} %bitcast.26), channel_id=1, source_target_pairs={{0,1},{1,2},{2,3},{3,0},{4,5},{5,6},{6,7},{7,4},{8,9},{9,10},{10,1... | collective-permute-start | bytes 393224 | tf_op jit(solution)/shard_map/ppermute | solution.py:44
  122.4 7.6 %collective-permute-start.17 = (bf16[4,128,128]{2,1,0:T(8,128)(2,1)S(1)}, bf16[4,128,128]{2,1,0:T(8,128)(2,1)S(1)}, u32[]{:S(2)}, u32[]{:S(2)}) collective-permute-start(bf16[4,128,128]{2,1,0:T(8,128)(2,1)S(1)} %get-tuple-element.28.refs_0_), channel_id=1, source_target_pairs={{0,192},{4,196},{8,200},{12,204},{16,208},{20,212},{24,216},{28,22... | collective-permute-start | bytes 393224 | tf_op jit(solution)/shard_map/ppermute | solution.py:39
  122.5 9.0 %collective-permute-start.18 = (bf16[4,128,128]{2,1,0:T(8,128)(2,1)S(1)}, bf16[4,128,128]{2,1,0:T(8,128)(2,1)S(1)}, u32[]{:S(2)}, u32[]{:S(2)}) collective-permute-start(bf16[4,128,128]{2,1,0:T(8,128)(2,1)S(1)} %get-tuple-element.28.refs_0_), channel_id=1, source_target_pairs={{0,128},{4,132},{8,136},{12,140},{16,144},{20,148},{24,152},{28,15... | collective-permute-start | bytes 393224 | tf_op jit(solution)/shard_map/ppermute | solution.py:39
  125.3 7.3 %collective-permute-start.19 = (bf16[4,128,128]{2,1,0:T(8,128)(2,1)S(1)}, bf16[4,128,128]{2,1,0:T(8,128)(2,1)S(1)}, u32[]{:S(2)}, u32[]{:S(2)}) collective-permute-start(bf16[4,128,128]{2,1,0:T(8,128)(2,1)S(1)} %get-tuple-element.28.refs_0_), channel_id=1, source_target_pairs={{0,64},{4,68},{8,72},{12,76},{16,80},{20,84},{24,88},{28,92},{32,9... | collective-permute-start | bytes 393224 | tf_op jit(solution)/shard_map/ppermute | solution.py:39
  126.4 9.8 %collective-permute-start.36 = (bf16[4,128,128]{2,1,0:T(8,128)(2,1)S(1)}, bf16[4,128,128]{2,1,0:T(8,128)(2,1)S(1)}, u32[]{:S(2)}, u32[]{:S(2)}) collective-permute-start(bf16[4,128,128]{2,1,0:T(8,128)(2,1)S(1)} %slice.87), channel_id=1, source_target_pairs={{0,32},{4,36},{8,40},{12,44},{16,48},{20,52},{24,56},{28,60},{32,0... | collective-permute-start | bytes 393224 | tf_op jit(solution)/shard_map/ppermute | solution.py:157
  132.6 51.8 %copy-start = (bf16[16,128,128]{2,1,0:T(8,128)(2,1)}, bf16[16,128,128]{2,1,0:T(8,128)(2,1)S(1)}, u32[]{:S(2)}) copy-start(bf16[16,128,128]{2,1,0:T(8,128)(2,1)S(1)} %join.3.rest_0_) | copy-start | bytes 1572868
  132.6 17.1 %collective-permute-start.20 = (bf16[16,128,128]{2,1,0:T(8,128)(2,1)S(1)}, bf16[16,128,128]{2,1,0:T(8,128)(2,1)S(1)}, u32[]{:S(2)}, u32[]{:S(2)}) collective-permute-start(bf16[16,128,128]{2,1,0:T(8,128)(2,1)S(1)} %join.3.rest_0_), channel_id=1, source_target_pairs={{0,56},{4,60},{8,0},{12,4},{16,8},{20,12},{24,16},{28,20},{32,24},... | collective-permute-start | bytes 1572872 | tf_op jit(solution)/shard_map/ppermute | solution.py:39
  132.9 19.0 %collective-permute-start.23 = (bf16[16,128,128]{2,1,0:T(8,128)(2,1)S(1)}, bf16[16,128,128]{2,1,0:T(8,128)(2,1)}, u32[]{:S(2)}, u32[]{:S(2)}) collective-permute-start(bf16[16,128,128]{2,1,0:T(8,128)(2,1)S(1)} %join.3.rest_0_), channel_id=1, source_target_pairs={{0,8},{4,12},{8,16},{12,20},{16,24},{20,28},{24,32},{28,36},{32,40... | collective-permute-start | bytes 1572872 | tf_op jit(solution)/shard_map/ppermute | solution.py:39
  136.4 6.5 %collective-permute-start.37 = (bf16[512,128]{1,0:T(8,128)(2,1)S(1)}, bf16[512,128]{1,0:T(8,128)(2,1)S(1)}, u32[]{:S(2)}, u32[]{:S(2)}) collective-permute-start(bf16[512,128]{1,0:T(8,128)(2,1)S(1)} %bitcast.29), channel_id=1, source_target_pairs={{0,3},{1,0},{2,1},{3,2},{4,7},{5,4},{6,5},{7,6},{8,11},{9,8},{10,9... | collective-permute-start | bytes 393224 | tf_op jit(solution)/shard_map/ppermute | solution.py:44
  139.0 6.6 %collective-permute-start.38 = (bf16[512,128]{1,0:T(8,128)(2,1)S(1)}, bf16[512,128]{1,0:T(8,128)(2,1)S(1)}, u32[]{:S(2)}, u32[]{:S(2)}) collective-permute-start(bf16[512,128]{1,0:T(8,128)(2,1)S(1)} %bitcast.30), channel_id=1, source_target_pairs={{0,2},{1,3},{2,0},{3,1},{4,6},{5,7},{6,4},{7,5},{8,10},{9,11},{10,... | collective-permute-start | bytes 393224 | tf_op jit(solution)/shard_map/ppermute | solution.py:44
  139.6 7.3 %collective-permute-start.39 = (bf16[512,128]{1,0:T(8,128)(2,1)S(1)}, bf16[512,128]{1,0:T(8,128)(2,1)S(1)}, u32[]{:S(2)}, u32[]{:S(2)}) collective-permute-start(bf16[512,128]{1,0:T(8,128)(2,1)S(1)} %bitcast.31), channel_id=1, source_target_pairs={{0,1},{1,2},{2,3},{3,0},{4,5},{5,6},{6,7},{7,4},{8,9},{9,10},{10,1... | collective-permute-start | bytes 393224 | tf_op jit(solution)/shard_map/ppermute | solution.py:44
  146.9 55.2 %copy-start.5 = (s32[1232]{0:T(1024)S(1)}, s32[1232]{0:T(1024)}, u32[]{:S(2)}) copy-start(s32[1232]{0:T(1024)} %plan.1.lists) | copy-start | bytes 14788
  149.7 2.3 %collective-permute-start.40 = (f32[512,128]{1,0:T(8,128)S(1)}, f32[512,128]{1,0:T(8,128)S(1)}, u32[]{:S(2)}, u32[]{:S(2)}) collective-permute-start(f32[512,128]{1,0:T(8,128)S(1)} %get-tuple-element.44), channel_id=1, source_target_pairs={{0,4},{4,0},{8,12},{12,8},{16,20},{20,16},{24,28},{28,24},{32,36},... | collective-permute-start | bytes 786440 | tf_op jit(solution)/shard_map/ppermute | solution.py:163
  149.8 52.2 %copy-start.15 = (bf16[16,128,128]{2,1,0:T(8,128)(2,1)}, bf16[16,128,128]{2,1,0:T(8,128)(2,1)S(1)}, u32[]{:S(2)}) copy-start(bf16[16,128,128]{2,1,0:T(8,128)(2,1)S(1)} %collective-permute-done.20.rest_1_) | copy-start | bytes 1572868
  149.8 14.3 %collective-permute-start.21 = (bf16[16,128,128]{2,1,0:T(8,128)(2,1)S(1)}, bf16[16,128,128]{2,1,0:T(8,128)(2,1)S(1)}, u32[]{:S(2)}, u32[]{:S(2)}) collective-permute-start(bf16[16,128,128]{2,1,0:T(8,128)(2,1)S(1)} %collective-permute-done.20.rest_1_), channel_id=1, source_target_pairs={{0,56},{4,60},{8,0},{12,4},{16,8},{20,12},{24,16},{28,20},{32,24},... | collective-permute-start | bytes 1572872 | tf_op jit(solution)/shard_map/ppermute | solution.py:39
  152.0 15.4 %collective-permute-start.24 = (bf16[16,128,128]{2,1,0:T(8,128)(2,1)}, bf16[16,128,128]{2,1,0:T(8,128)(2,1)S(1)}, u32[]{:S(2)}, u32[]{:S(2)}) collective-permute-start(bf16[16,128,128]{2,1,0:T(8,128)(2,1)} %collective-permute-done.23.rest_6_), channel_id=1, source_target_pairs={{0,8},{4,12},{8,16},{12,20},{16,24},{20,28},{24,32},{28,36},{32,40... | collective-permute-start | bytes 1572872 | tf_op jit(solution)/shard_map/ppermute | solution.py:39
  152.0 15.4 %collective-permute-start.41 = (f32[256,128]{1,0:T(8,128)S(1)}, f32[256,128]{1,0:T(8,128)S(1)}, u32[]{:S(2)}, u32[]{:S(2)}) collective-permute-start(f32[256,128]{1,0:T(8,128)S(1)} %slice_select_fusion), channel_id=1, source_target_pairs={{0,64},{4,68},{8,72},{12,76},{16,80},{20,84},{24,88},{28,92},{32,9... | collective-permute-start | bytes 393224 | tf_op jit(solution)/shard_map/ppermute | solution.py:169
  164.1 37.9 %copy-start.16 = (bf16[16,128,128]{2,1,0:T(8,128)(2,1)}, bf16[16,128,128]{2,1,0:T(8,128)(2,1)S(1)}, u32[]{:S(2)}) copy-start(bf16[16,128,128]{2,1,0:T(8,128)(2,1)S(1)} %collective-permute-done.21.rest_2_) | copy-start | bytes 1572868
  164.1 20.3 %collective-permute-start.22 = (bf16[16,128,128]{2,1,0:T(8,128)(2,1)S(1)}, bf16[16,128,128]{2,1,0:T(8,128)(2,1)S(1)}, u32[]{:S(2)}, u32[]{:S(2)}) collective-permute-start(bf16[16,128,128]{2,1,0:T(8,128)(2,1)S(1)} %collective-permute-done.21.rest_2_), channel_id=1, source_target_pairs={{0,56},{4,60},{8,0},{12,4},{16,8},{20,12},{24,16},{28,20},{32,24},... | collective-permute-start | bytes 1572872 | tf_op jit(solution)/shard_map/ppermute | solution.py:39
  167.4 34.6 %copy-start.17 = (bf16[16,128,128]{2,1,0:T(8,128)(2,1)}, bf16[16,128,128]{2,1,0:T(8,128)(2,1)S(1)}, u32[]{:S(2)}) copy-start(bf16[16,128,128]{2,1,0:T(8,128)(2,1)S(1)} %collective-permute-done.24.rest_5_) | copy-start | bytes 1572868
  167.4 14.4 %collective-permute-start.25 = (bf16[16,128,128]{2,1,0:T(8,128)(2,1)S(1)}, bf16[16,128,128]{2,1,0:T(8,128)(2,1)S(1)}, u32[]{:S(2)}, u32[]{:S(2)}) collective-permute-start(bf16[16,128,128]{2,1,0:T(8,128)(2,1)S(1)} %collective-permute-done.24.rest_5_), channel_id=1, source_target_pairs={{0,8},{4,12},{8,16},{12,20},{16,24},{20,28},{24,32},{28,36},{32,40... | collective-permute-start | bytes 1572872 | tf_op jit(solution)/shard_map/ppermute | solution.py:39
  167.5 6.6 %collective-permute-start.42 = (f32[256,128]{1,0:T(8,128)S(1)}, f32[256,128]{1,0:T(8,128)S(1)}, u32[]{:S(2)}, u32[]{:S(2)}) collective-permute-start(f32[256,128]{1,0:T(8,128)S(1)} %select_add_fusion), channel_id=1, source_target_pairs={{0,128},{4,132},{8,136},{12,140},{16,144},{20,148},{24,152},{28,15... | collective-permute-start | bytes 393224 | tf_op jit(solution)/shard_map/ppermute | solution.py:171
  174.0 7.7 %collective-permute-start.43 = (f32[256,128]{1,0:T(8,128)S(1)}, f32[256,128]{1,0:T(8,128)S(1)}, u32[]{:S(2)}, u32[]{:S(2)}) collective-permute-start(f32[256,128]{1,0:T(8,128)S(1)} %add.59), channel_id=1, source_target_pairs={{0,8},{4,12},{8,0},{12,4},{16,24},{20,28},{24,16},{28,20},{32,40},... | collective-permute-start | bytes 393224 | tf_op jit(solution)/shard_map/ppermute | solution.py:171
  181.7 9.3 %collective-permute-start.44 = (f32[256,128]{1,0:T(8,128)S(1)}, f32[256,128]{1,0:T(8,128)S(1)}, u32[]{:S(2)}, u32[]{:S(2)}) collective-permute-start(f32[256,128]{1,0:T(8,128)S(1)} %add.60), channel_id=1, source_target_pairs={{0,16},{4,20},{8,24},{12,28},{16,0},{20,4},{24,8},{28,12},{32,48},... | collective-permute-start | bytes 393224 | tf_op jit(solution)/shard_map/ppermute | solution.py:171
  181.8 20.2 %copy-start.12 = (bf16[16,128,128]{2,1,0:T(8,128)(2,1)}, bf16[16,128,128]{2,1,0:T(8,128)(2,1)S(1)}, u32[]{:S(2)}) copy-start(bf16[16,128,128]{2,1,0:T(8,128)(2,1)S(1)} %collective-permute-done.25.rest_4_) | copy-start | bytes 1572868
  181.9 27.6 %collective-permute-start.26 = (bf16[8,128,128]{2,1,0:T(8,128)(2,1)S(1)}, bf16[8,128,128]{2,1,0:T(8,128)(2,1)S(1)}, u32[]{:S(2)}, u32[]{:S(2)}) collective-permute-start(bf16[8,128,128]{2,1,0:T(8,128)(2,1)S(1)} %slice.64), channel_id=1, source_target_pairs={{0,8},{4,12},{8,16},{12,20},{16,24},{20,28},{24,32},{28,36},{32,40... | collective-permute-start | bytes 786440 | tf_op jit(solution)/shard_map/ppermute | solution.py:39
  184.4 17.6 %copy-start.11 = (bf16[16,128,128]{2,1,0:T(8,128)(2,1)}, bf16[16,128,128]{2,1,0:T(8,128)(2,1)S(1)}, u32[]{:S(2)}) copy-start(bf16[16,128,128]{2,1,0:T(8,128)(2,1)S(1)} %collective-permute-done.22.rest_3_) | copy-start | bytes 1572868
  184.5 25.0 %collective-permute-start.27 = (bf16[8,128,128]{2,1,0:T(8,128)(2,1)S(1)}, bf16[8,128,128]{2,1,0:T(8,128)(2,1)S(1)}, u32[]{:S(2)}, u32[]{:S(2)}) collective-permute-start(bf16[8,128,128]{2,1,0:T(8,128)(2,1)S(1)} %slice.65), channel_id=1, source_target_pairs={{0,56},{4,60},{8,0},{12,4},{16,8},{20,12},{24,16},{28,20},{32,24},... | collective-permute-start | bytes 786440 | tf_op jit(solution)/shard_map/ppermute | solution.py:39
  191.0 10.7 %collective-permute-start.45 = (f32[256,128]{1,0:T(8,128)S(1)}, f32[256,128]{1,0:T(8,128)S(1)}, u32[]{:S(2)}, u32[]{:S(2)}) collective-permute-start(f32[256,128]{1,0:T(8,128)S(1)} %add.61), channel_id=1, source_target_pairs={{0,32},{4,36},{8,40},{12,44},{16,48},{20,52},{24,56},{28,60},{32,0... | collective-permute-start | bytes 393224 | tf_op jit(solution)/shard_map/ppermute | solution.py:171
  201.7 11.1 %collective-permute-start.46 = (f32[256,128]{1,0:T(8,128)S(1)}, f32[256,128]{1,0:T(8,128)S(1)}, u32[]{:S(2)}, u32[]{:S(2)}) collective-permute-start(f32[256,128]{1,0:T(8,128)S(1)} %add.62), channel_id=1, source_target_pairs={{0,64},{4,68},{8,72},{12,76},{16,80},{20,84},{24,88},{28,92},{32,9... | collective-permute-start | bytes 393224 | tf_op jit(solution)/shard_map/ppermute | solution.py:178
  212.7 1.6 collective-permute-start.28
  212.8 2.1 collective-permute-start.47
  (8 other events, 21.5 us)
where the time goes:
time: 219 us; the launch traced here: 216 us
  waiting for transfers between devices  100 us (46%)
  starting transfers between devices  64.8 us (30%)
  Pallas kernels  41.4 us (19%)
  local copies, waits for them, and re-layouts  5.37 us (2%)
  other arithmetic  3.51 us (2%)
    ppermute x31, waiting for transfers between devices, send(): return lax.ppermute(value, 'nodes', node_pairs(dx, dz, dc))  58.6 us
    ppermute x31, starting transfers between devices, send(): return lax.ppermute(value, 'nodes', node_pairs(dx, dz, dc))  40.3 us
    ppermute x4, waiting for transfers between devices, halve(): value = value + lax.ppermute(value, 'nodes', xor_pairs(bit))  25.2 us
    pallas_call x2, Pallas kernels, early_call(): pl.pallas_call(kernel, out_shape=[shape, shape], in_specs=[smem] + [free]...  14.8 us
    ppermute x6, waiting for transfers between devices, gather_y(): lax.ppermute(value, 'feat', pairs[r])  14.8 us
    pallas_call x1, Pallas kernels, transposed_terms(): pl.pallas_call(transposed_kernel, out_shape=[shape] * NX, in_specs=[smem,...  8.48 us
    ppermute x6, starting transfers between devices, gather_y(): lax.ppermute(value, 'feat', pairs[r])  8.43 us
    ppermute x2, starting transfers between devices, reduce_plane(): lax.ppermute(give, 'nodes', xor_pairs(bit * NC)).astype(f32)  6.64 us
  transfers between devices with their start and end apart: 48, of which 24 were waited for; matrix products, arithmetic and copies ran while one was open for 2% of the time, Pallas kernels for 15%

commit v1 on v0

--- a/solution.py
+++ b/solution.py
@@ -409,15 +409,15 @@
         for s, out in ((0, out_a), (1, out_b)):
 
             def some(i, carry, s=s, out=out):
-                for j in range(2):
-                    k = i * 2 + j
+                for j in range(LATE // 2):
+                    k = i * (LATE // 2) + j
                     at = late + 2 * LATE * s + k
                     term = jnp.dot(got[s * LATE + k], held[lists[at + 4 * LATE]], preferred_element_type=jnp.float32)
                     row = lists[at + 8 * LATE]
                     out[row] = out[row] + term
                 return carry
 
-            lax.fori_loop(0, LATE // 2, some, 0)
+            lax.fori_loop(0, 2, some, 0)
 
     shape = jax.ShapeDtypeStruct((rows, blk, width), jnp.float32)
     smem = pl.BlockSpec(memory_space=pltpu.SMEM)

time: 219 us -> 217 us (level)
  no operation moved by 1% of the time
where the time goes in v1:
time: 217 us; the launch traced here: 215 us
  waiting for transfers between devices  100 us (46%)
  starting transfers between devices  64.8 us (30%)
  Pallas kernels  40.2 us (19%)
  local copies, waits for them, and re-layouts  5.37 us (2%)
  other arithmetic  3.51 us (2%)
    ppermute x31, waiting for transfers between devices, send(): return lax.ppermute(value, 'nodes', node_pairs(dx, dz, dc))  58.7 us
    ppermute x31, starting transfers between devices, send(): return lax.ppermute(value, 'nodes', node_pairs(dx, dz, dc))  40.2 us
    ppermute x4, waiting for transfers between devices, halve(): value = value + lax.ppermute(value, 'nodes', xor_pairs(bit))  24.9 us
    ppermute x6, waiting for transfers between devices, gather_y(): lax.ppermute(value, 'feat', pairs[r])  14.8 us
    pallas_call x2, Pallas kernels, early_call(): pl.pallas_call(kernel, out_shape=[shape, shape], in_specs=[smem] + [free]...  14.8 us
    pallas_call x1, Pallas kernels, transposed_terms(): pl.pallas_call(transposed_kernel, out_shape=[shape] * NX, in_specs=[smem,...  8.48 us
    ppermute x6, starting transfers between devices, gather_y(): lax.ppermute(value, 'feat', pairs[r])  8.37 us
    ppermute x2, starting transfers between devices, reduce_plane(): lax.ppermute(give, 'nodes', xor_pairs(bit * NC)).astype(f32)  6.56 us
  transfers between devices with their start and end apart: 48, of which 24 were waited for; matrix products, arithmetic and copies ran while one was open for 2% of the time, Pallas kernels for 15%

profile of v1, /device:TPU:2, one launch (start us, length us, event | category | flops | bytes accessed | tf_op | source)
XLA Modules:
  0.0 215.1 jit_solution(3849479355564896315)
XLA Ops:
  1.2 0.7 add_bitcast_fusion.col_a
  2.6 4.2 %collective-permute-done.col_b = s32[96]{0:T(128)S(1)} collective-permute-done((s32[96]{0:T(128)S(1)}, s32[96]{0:T(128)S(1)}, u32[]{:S(2)}, u32[]{:S(2)}) %collective-permute-start) | collective-permute-done | bytes 416 | tf_op jit(solution)/shard_map/ppermute | solution.py:39
  7.3 5.9 %plan.1.lists = s32[1232]{0:T(1024)} custom-call(s32[4]{0:T(128)} %pad_add_fusion.place, s32[96]{0:T(128)} %copy-done.22, s32[96]{0:T(128)} %copy-done.23), custom_call_target="tpu_custom_call" | custom-call | tf_op jit(solution)/shard_map/plan/pallas_call | solution.py:245
  13.2 1.6 copy-done.9
  14.9 0.7 copy-done.4
  15.5 0.9 copy-done.6
  16.5 8.5 %transposed_terms.1 = (bf16[32,128,128]{2,1,0:T(8,128)(2,1)S(1)}, bf16[32,128,128]{2,1,0:T(8,128)(2,1)S(1)}, bf16[32,128,128]{2,1,0:T(8,128)(2,1)S(1)}, bf16[32,128,128]{2,1,0:T(8,128)(2,1)S(1)}) custom-call(s32[1232]{0:T(1024)S(1)} %copy-done.4, bf16[96,128,128]{2,1,0:T(8,128)(2,1)} %bitcast.38, bf16[96,128,128]{2,1,0:T(8,128)(2,1)} %copy-done.9, ...), custom_call_target="tpu_custom_call" | custom-call | tf_op jit(solution)/shard_map/transposed_terms/pallas_call | solution.py:307
  25.0 1.6 collective-permute-start.30
  26.6 0.8 collective-permute-start.31
  27.4 3.1 %collective-permute-start.2 = (bf16[4,128,128]{2,1,0:T(8,128)(2,1)S(1)}, bf16[4,128,128]{2,1,0:T(8,128)(2,1)S(1)}, u32[]{:S(2)}, u32[]{:S(2)}) collective-permute-start(bf16[4,128,128]{2,1,0:T(8,128)(2,1)S(1)} %bitcast.33), channel_id=1, source_target_pairs={{0,192},{4,196},{8,200},{12,204},{16,208},{20,212},{24,216},{28,22... | collective-permute-start | bytes 393224 | tf_op jit(solution)/shard_map/ppermute | solution.py:39
  30.6 1.5 collective-permute-start.4
  32.1 11.2 %collective-permute-done.2.refs_1_ = bf16[4,128,128]{2,1,0:T(8,128)(2,1)S(1)} collective-permute-done((bf16[4,128,128]{2,1,0:T(8,128)(2,1)S(1)}, bf16[4,128,128]{2,1,0:T(8,128)(2,1)S(1)}, u32[]{:S(2)}, u32[]{:S(2)}) %collective-permute-start.2) | collective-permute-done | bytes 131104 | tf_op jit(solution)/shard_map/ppermute | solution.py:39
  43.3 2.6 %collective-permute-done.3.refs_2_ = bf16[4,128,128]{2,1,0:T(8,128)(2,1)S(1)} collective-permute-done((bf16[4,128,128]{2,1,0:T(8,128)(2,1)S(1)}, bf16[4,128,128]{2,1,0:T(8,128)(2,1)S(1)}, u32[]{:S(2)}, u32[]{:S(2)}) %collective-permute-start.3) | collective-permute-done | bytes 131104 | tf_op jit(solution)/shard_map/ppermute | solution.py:39
  45.9 2.0 collective-permute-start.8
  47.9 3.6 %collective-permute-start.5 = (bf16[16,128,128]{2,1,0:T(8,128)(2,1)S(1)}, bf16[16,128,128]{2,1,0:T(8,128)(2,1)S(1)}, u32[]{:S(2)}, u32[]{:S(2)}) collective-permute-start(bf16[16,128,128]{2,1,0:T(8,128)(2,1)S(1)} %join.2.rest_0_), channel_id=1, source_target_pairs={{0,56},{4,60},{8,0},{12,4},{16,8},{20,12},{24,16},{28,20},{32,24},... | collective-permute-start | bytes 1572872 | tf_op jit(solution)/shard_map/ppermute | solution.py:39
  51.9 2.0 collective-permute-start.33
  53.9 7.4 %collective-permute-done.8.rest_6_ = bf16[16,128,128]{2,1,0:T(8,128)(2,1)S(1)} collective-permute-done((bf16[16,128,128]{2,1,0:T(8,128)(2,1)S(1)}, bf16[16,128,128]{2,1,0:T(8,128)(2,1)S(1)}, u32[]{:S(2)}, u32[]{:S(2)}) %collective-permute-start.8) | collective-permute-done | bytes 524320 | tf_op jit(solution)/shard_map/ppermute | solution.py:39
  61.3 3.2 %collective-permute-start.6 = (bf16[16,128,128]{2,1,0:T(8,128)(2,1)S(1)}, bf16[16,128,128]{2,1,0:T(8,128)(2,1)S(1)}, u32[]{:S(2)}, u32[]{:S(2)}) collective-permute-start(bf16[16,128,128]{2,1,0:T(8,128)(2,1)S(1)} %collective-permute-done.5.rest_1_), channel_id=1, source_target_pairs={{0,56},{4,60},{8,0},{12,4},{16,8},{20,12},{24,16},{28,20},{32,24},... | collective-permute-start | bytes 1572872 | tf_op jit(solution)/shard_map/ppermute | solution.py:39
  64.5 9.0 %collective-permute-done.9.rest_5_ = bf16[16,128,128]{2,1,0:T(8,128)(2,1)S(1)} collective-permute-done((bf16[16,128,128]{2,1,0:T(8,128)(2,1)S(1)}, bf16[16,128,128]{2,1,0:T(8,128)(2,1)S(1)}, u32[]{:S(2)}, u32[]{:S(2)}) %collective-permute-start.9) | collective-permute-done | bytes 524320 | tf_op jit(solution)/shard_map/ppermute | solution.py:39
  73.6 3.2 %collective-permute-start.7 = (bf16[16,128,128]{2,1,0:T(8,128)(2,1)S(1)}, bf16[16,128,128]{2,1,0:T(8,128)(2,1)S(1)}, u32[]{:S(2)}, u32[]{:S(2)}) collective-permute-start(bf16[16,128,128]{2,1,0:T(8,128)(2,1)S(1)} %collective-permute-done.6.rest_2_), channel_id=1, source_target_pairs={{0,56},{4,60},{8,0},{12,4},{16,8},{20,12},{24,16},{28,20},{32,24},... | collective-permute-start | bytes 1572872 | tf_op jit(solution)/shard_map/ppermute | solution.py:39
  77.4 8.5 %collective-permute-done.10.rest_4_ = bf16[16,128,128]{2,1,0:T(8,128)(2,1)S(1)} collective-permute-done((bf16[16,128,128]{2,1,0:T(8,128)(2,1)S(1)}, bf16[16,128,128]{2,1,0:T(8,128)(2,1)S(1)}, u32[]{:S(2)}, u32[]{:S(2)}) %collective-permute-start.10) | collective-permute-done | bytes 524320 | tf_op jit(solution)/shard_map/ppermute | solution.py:39
  85.9 2.6 %collective-permute-start.11 = (bf16[8,128,128]{2,1,0:T(8,128)(2,1)S(1)}, bf16[8,128,128]{2,1,0:T(8,128)(2,1)S(1)}, u32[]{:S(2)}, u32[]{:S(2)}) collective-permute-start(bf16[8,128,128]{2,1,0:T(8,128)(2,1)S(1)} %slice.62), channel_id=1, source_target_pairs={{0,8},{4,12},{8,16},{12,20},{16,24},{20,28},{24,32},{28,36},{32,40... | collective-permute-start | bytes 786440 | tf_op jit(solution)/shard_map/ppermute | solution.py:39
  88.7 1.9 collective-permute-start.12
  90.6 7.4 %early.2 = (f32[4,128,128]{2,1,0:T(8,128)S(1)}, f32[4,128,128]{2,1,0:T(8,128)S(1)}) custom-call(s32[1232]{0:T(1024)S(1)} %copy-done.4, bf16[96,128,128]{2,1,0:T(8,128)(2,1)} %bitcast.39, bf16[96,128,128]{2,1,0:T(8,128)(2,1)} %copy-done.9, bf16[16,128,128]{2,1,0:T(8,128)(2,1)} %copy-done.1, bf16[16,128,128]{2,1,0:T(8,128)(2,1)} %copy-done.19, ...), custom_call_target="tpu_custom_call" | custom-call | tf_op jit(solution)/shard_map/early/pallas_call | solution.py:369
  98.4 2.5 %collective-permute-done.12.rest_1_ = bf16[8,128,128]{2,1,0:T(8,128)(2,1)S(1)} collective-permute-done((bf16[8,128,128]{2,1,0:T(8,128)(2,1)S(1)}, bf16[8,128,128]{2,1,0:T(8,128)(2,1)S(1)}, u32[]{:S(2)}, u32[]{:S(2)}) %collective-permute-start.12) | collective-permute-done | bytes 262176 | tf_op jit(solution)/shard_map/ppermute | solution.py:39
  100.9 2.6 %late.2 = (f32[4,128,128]{2,1,0:T(8,128)S(1)}, f32[4,128,128]{2,1,0:T(8,128)S(1)}) custom-call(s32[1232]{0:T(1024)S(1)} %copy-done.4, bf16[96,128,128]{2,1,0:T(8,128)(2,1)} %bitcast.40, bf16[96,128,128]{2,1,0:T(8,128)(2,1)} %copy-done.9, f32[4,128,128]{2,1,0:T(8,128)S(1)} %get-tuple-element.24.early_a, f32[4,128,128]{2,1,0:T(8,128)S(1)} %get-tuple-element.25.early_b, ...), custom_call_target="tpu_custom_call" | custom-call | tf_op jit(solution)/shard_map/late/pallas_call | solution.py:427
  103.8 3.0 %collective-permute-start.35 = (bf16[8,128,128]{2,1,0:T(8,128)(2,1)S(1)}, bf16[8,128,128]{2,1,0:T(8,128)(2,1)S(1)}, u32[]{:S(2)}, u32[]{:S(2)}) collective-permute-start(bf16[8,128,128]{2,1,0:T(8,128)(2,1)S(1)} %slice.86), channel_id=1, source_target_pairs={{0,16},{4,20},{8,24},{12,28},{16,0},{20,4},{24,8},{28,12},{32,48},... | collective-permute-start | bytes 786440 | tf_op jit(solution)/shard_map/ppermute | solution.py:157
  106.8 3.1 %collective-permute-start.14 = (bf16[512,128]{1,0:T(8,128)(2,1)S(1)}, bf16[512,128]{1,0:T(8,128)(2,1)S(1)}, u32[]{:S(2)}, u32[]{:S(2)}) collective-permute-start(bf16[512,128]{1,0:T(8,128)(2,1)S(1)} %bitcast.24), channel_id=1, source_target_pairs={{0,3},{1,0},{2,1},{3,2},{4,7},{5,4},{6,5},{7,6},{8,11},{9,8},{10,9... | collective-permute-start | bytes 393224 | tf_op jit(solution)/shard_map/ppermute | solution.py:44
  109.9 0.6 collective-permute-start.15
  110.6 1.0 collective-permute-start.16
  111.6 4.3 %collective-permute-done.14.p1 = bf16[512,128]{1,0:T(8,128)(2,1)S(1)} collective-permute-done((bf16[512,128]{1,0:T(8,128)(2,1)S(1)}, bf16[512,128]{1,0:T(8,128)(2,1)S(1)}, u32[]{:S(2)}, u32[]{:S(2)}) %collective-permute-start.14) | collective-permute-done | bytes 131104 | tf_op jit(solution)/shard_map/ppermute | solution.py:44
  115.9 2.0 collective-permute-done.15.p2
  117.8 1.7 collective-permute-done.16.p3
  119.6 2.3 %mixing.1 = (f32[512,512]{1,0:T(8,128)S(1)}, bf16[512,128]{1,0:T(8,128)(2,1)S(1)}, bf16[4,128,128]{2,1,0:T(8,128)(2,1)S(1)}) custom-call(s32[4]{0:T(128)S(1)} %copy-done.8, bf16[512,128]{1,0:T(8,128)(2,1)S(1)} %bitcast.27, bf16[512,128]{1,0:T(8,128)(2,1)S(1)} %collective-permute-done.14.p1, bf16[512,128]{1,0:T(8,128)(2,1)S(1)} %collective-permute-done.15.p2, ...), custom_call_target="tpu_custom_call" | custom-call | tf_op jit(solution)/shard_map/mixing/pallas_call | solution.py:469
  122.0 2.7 %collective-permute-start.18 = (bf16[4,128,128]{2,1,0:T(8,128)(2,1)S(1)}, bf16[4,128,128]{2,1,0:T(8,128)(2,1)S(1)}, u32[]{:S(2)}, u32[]{:S(2)}) collective-permute-start(bf16[4,128,128]{2,1,0:T(8,128)(2,1)S(1)} %get-tuple-element.28.refs_0_), channel_id=1, source_target_pairs={{0,128},{4,132},{8,136},{12,140},{16,144},{20,148},{24,152},{28,15... | collective-permute-start | bytes 393224 | tf_op jit(solution)/shard_map/ppermute | solution.py:39
  124.7 1.1 slice_add_fusion
  125.8 3.6 %collective-permute-start.36 = (bf16[4,128,128]{2,1,0:T(8,128)(2,1)S(1)}, bf16[4,128,128]{2,1,0:T(8,128)(2,1)S(1)}, u32[]{:S(2)}, u32[]{:S(2)}) collective-permute-start(bf16[4,128,128]{2,1,0:T(8,128)(2,1)S(1)} %slice.87), channel_id=1, source_target_pairs={{0,32},{4,36},{8,40},{12,44},{16,48},{20,52},{24,56},{28,60},{32,0... | collective-permute-start | bytes 393224 | tf_op jit(solution)/shard_map/ppermute | solution.py:157
  129.4 1.4 collective-permute-done.18.refs_2_
  130.9 1.1 collective-permute-done.19.refs_3_
  132.3 1.8 collective-permute-start.23
  134.2 1.5 collective-permute-done.36
  135.8 2.6 %collective-permute-start.37 = (bf16[512,128]{1,0:T(8,128)(2,1)S(1)}, bf16[512,128]{1,0:T(8,128)(2,1)S(1)}, u32[]{:S(2)}, u32[]{:S(2)}) collective-permute-start(bf16[512,128]{1,0:T(8,128)(2,1)S(1)} %bitcast.29), channel_id=1, source_target_pairs={{0,3},{1,0},{2,1},{3,2},{4,7},{5,4},{6,5},{7,6},{8,11},{9,8},{10,9... | collective-permute-start | bytes 393224 | tf_op jit(solution)/shard_map/ppermute | solution.py:44
  139.5 2.8 %collective-permute-done.37.q1 = bf16[512,128]{1,0:T(8,128)(2,1)S(1)} collective-permute-done((bf16[512,128]{1,0:T(8,128)(2,1)S(1)}, bf16[512,128]{1,0:T(8,128)(2,1)S(1)}, u32[]{:S(2)}, u32[]{:S(2)}) %collective-permute-start.37) | collective-permute-done | bytes 131104 | tf_op jit(solution)/shard_map/ppermute | solution.py:44
  142.4 2.6 %collective-permute-done.38.q2 = bf16[512,128]{1,0:T(8,128)(2,1)S(1)} collective-permute-done((bf16[512,128]{1,0:T(8,128)(2,1)S(1)}, bf16[512,128]{1,0:T(8,128)(2,1)S(1)}, u32[]{:S(2)}, u32[]{:S(2)}) %collective-permute-start.38) | collective-permute-done | bytes 131104 | tf_op jit(solution)/shard_map/ppermute | solution.py:44
  145.0 1.3 collective-permute-done.39.q3
  146.3 2.8 %grads.1 = (f32[512,128]{1,0:T(8,128)S(1)}, f32[512,128]{1,0:T(8,128)S(1)}) custom-call(s32[4]{0:T(128)S(1)} %copy-done.8, f32[512,512]{1,0:T(8,128)S(1)} %get-tuple-element.33.z_all, bf16[512,128]{1,0:T(8,128)(2,1)S(1)} %bitcast.28, bf16[512,128]{1,0:T(8,128)(2,1)S(1)} %get-tuple-element.34.own, bf16[512,128]{1,0:T(8,128)(2,1)S(1)} %bitcast.32, ...), custom_call_target="tpu_custom_call" | custom-call | tf_op jit(solution)/shard_map/grads/pallas_call | solution.py:521
  149.3 2.1 collective-permute-start.21
  151.4 2.8 %collective-permute-start.41 = (f32[256,128]{1,0:T(8,128)S(1)}, f32[256,128]{1,0:T(8,128)S(1)}, u32[]{:S(2)}, u32[]{:S(2)}) collective-permute-start(f32[256,128]{1,0:T(8,128)S(1)} %slice_select_fusion), channel_id=1, source_target_pairs={{0,64},{4,68},{8,72},{12,76},{16,80},{20,84},{24,88},{28,92},{32,9... | collective-permute-start | bytes 393224 | tf_op jit(solution)/shard_map/ppermute | solution.py:169
  154.3 9.3 %collective-permute-done.21.rest_2_ = bf16[16,128,128]{2,1,0:T(8,128)(2,1)S(1)} collective-permute-done((bf16[16,128,128]{2,1,0:T(8,128)(2,1)S(1)}, bf16[16,128,128]{2,1,0:T(8,128)(2,1)S(1)}, u32[]{:S(2)}, u32[]{:S(2)}) %collective-permute-start.21) | collective-permute-done | bytes 524320 | tf_op jit(solution)/shard_map/ppermute | solution.py:39
  163.6 3.2 %collective-permute-start.22 = (bf16[16,128,128]{2,1,0:T(8,128)(2,1)S(1)}, bf16[16,128,128]{2,1,0:T(8,128)(2,1)S(1)}, u32[]{:S(2)}, u32[]{:S(2)}) collective-permute-start(bf16[16,128,128]{2,1,0:T(8,128)(2,1)S(1)} %collective-permute-done.21.rest_2_), channel_id=1, source_target_pairs={{0,56},{4,60},{8,0},{12,4},{16,8},{20,12},{24,16},{28,20},{32,24},... | collective-permute-start | bytes 1572872 | tf_op jit(solution)/shard_map/ppermute | solution.py:39
  166.8 3.1 %collective-permute-start.42 = (f32[256,128]{1,0:T(8,128)S(1)}, f32[256,128]{1,0:T(8,128)S(1)}, u32[]{:S(2)}, u32[]{:S(2)}) collective-permute-start(f32[256,128]{1,0:T(8,128)S(1)} %select_add_fusion), channel_id=1, source_target_pairs={{0,128},{4,132},{8,136},{12,140},{16,144},{20,148},{24,152},{28,15... | collective-permute-start | bytes 393224 | tf_op jit(solution)/shard_map/ppermute | solution.py:171
  169.9 3.5 %collective-permute-done.42 = f32[256,128]{1,0:T(8,128)S(1)} collective-permute-done((f32[256,128]{1,0:T(8,128)S(1)}, f32[256,128]{1,0:T(8,128)S(1)}, u32[]{:S(2)}, u32[]{:S(2)}) %collective-permute-start.42) | collective-permute-done | bytes 131104 | tf_op jit(solution)/shard_map/ppermute | solution.py:171
  173.5 7.6 %collective-permute-done.43 = f32[256,128]{1,0:T(8,128)S(1)} collective-permute-done((f32[256,128]{1,0:T(8,128)S(1)}, f32[256,128]{1,0:T(8,128)S(1)}, u32[]{:S(2)}, u32[]{:S(2)}) %collective-permute-start.43) | collective-permute-done | bytes 131104 | tf_op jit(solution)/shard_map/ppermute | solution.py:171
  181.3 2.6 %collective-permute-start.26 = (bf16[8,128,128]{2,1,0:T(8,128)(2,1)S(1)}, bf16[8,128,128]{2,1,0:T(8,128)(2,1)S(1)}, u32[]{:S(2)}, u32[]{:S(2)}) collective-permute-start(bf16[8,128,128]{2,1,0:T(8,128)(2,1)S(1)} %slice.64), channel_id=1, source_target_pairs={{0,8},{4,12},{8,16},{12,20},{16,24},{20,28},{24,32},{28,36},{32,40... | collective-permute-start | bytes 786440 | tf_op jit(solution)/shard_map/ppermute | solution.py:39
  183.9 0.8 collective-permute-start.27
  184.7 5.6 %collective-permute-done.44 = f32[256,128]{1,0:T(8,128)S(1)} collective-permute-done((f32[256,128]{1,0:T(8,128)S(1)}, f32[256,128]{1,0:T(8,128)S(1)}, u32[]{:S(2)}, u32[]{:S(2)}) %collective-permute-start.44) | collective-permute-done | bytes 131104 | tf_op jit(solution)/shard_map/ppermute | solution.py:171
  190.4 1.6 collective-permute-start.45
  192.0 8.2 %collective-permute-done.45 = f32[256,128]{1,0:T(8,128)S(1)} collective-permute-done((f32[256,128]{1,0:T(8,128)S(1)}, f32[256,128]{1,0:T(8,128)S(1)}, u32[]{:S(2)}, u32[]{:S(2)}) %collective-permute-start.45) | collective-permute-done | bytes 131104 | tf_op jit(solution)/shard_map/ppermute | solution.py:171
  200.2 1.2 collective-permute-start.46
  201.4 7.4 %early.3 = (f32[4,128,128]{2,1,0:T(8,128)S(1)}, f32[4,128,128]{2,1,0:T(8,128)S(1)}) custom-call(s32[1232]{0:T(1024)S(1)} %copy-done.5, bf16[96,128,128]{2,1,0:T(8,128)(2,1)} %bitcast.41, bf16[96,128,128]{2,1,0:T(8,128)(2,1)} %copy-done.9, bf16[16,128,128]{2,1,0:T(8,128)(2,1)} %copy-done, bf16[16,128,128]{2,1,0:T(8,128)(2,1)} %copy-done.15, ...), custom_call_target="tpu_custom_call" | custom-call | tf_op jit(solution)/shard_map/early/pallas_call | solution.py:369
  208.9 2.6 %late.3 = (f32[4,128,128]{2,1,0:T(8,128)S(1)}, f32[4,128,128]{2,1,0:T(8,128)S(1)}) custom-call(s32[1232]{0:T(1024)S(1)} %copy-done.5, bf16[96,128,128]{2,1,0:T(8,128)(2,1)} %bitcast.42, bf16[96,128,128]{2,1,0:T(8,128)(2,1)} %copy-done.9, f32[4,128,128]{2,1,0:T(8,128)S(1)} %get-tuple-element.29.early_a, f32[4,128,128]{2,1,0:T(8,128)S(1)} %get-tuple-element.30.early_b, ...), custom_call_target="tpu_custom_call" | custom-call | tf_op jit(solution)/shard_map/late/pallas_call | solution.py:427
  212.2 0.9 collective-permute-done.28
  213.1 0.7 add_convert_fusion
  214.3 0.8 copy_bitcast_fusion
  (123 shorter events, 7.2 us)
Async XLA Ops:
  0.6 12.6 %collective-permute-start.1 = (bf16[96,128,128]{2,1,0:T(8,128)(2,1)}, bf16[96,128,128]{2,1,0:T(8,128)(2,1)S(1)}, u32[]{:S(2)}, u32[]{:S(2)}) collective-permute-start(bf16[96,128,128]{2,1,0:T(8,128)(2,1)} %bitcast.37), channel_id=1, source_target_pairs={{0,4},{4,0},{8,12},{12,8},{16,20},{20,16},{24,28},{28,24},{32,36},... | collective-permute-start | bytes 9437192 | tf_op jit(solution)/shard_map/ppermute | solution.py:39
  0.7 12.5 %collective-permute-start.29 = (bf16[512,128]{1,0:T(8,128)(2,1)}, bf16[512,128]{1,0:T(8,128)(2,1)S(1)}, u32[]{:S(2)}, u32[]{:S(2)}) collective-permute-start(bf16[512,128]{1,0:T(8,128)(2,1)} %cot_a.1), channel_id=1, source_target_pairs={{0,4},{4,0},{8,12},{12,8},{16,20},{20,16},{24,28},{28,24},{32,36},... | collective-permute-start | bytes 393224 | tf_op jit(solution)/shard_map/ppermute | solution.py:39
  1.9 4.9 %collective-permute-start = (s32[96]{0:T(128)S(1)}, s32[96]{0:T(128)S(1)}, u32[]{:S(2)}, u32[]{:S(2)}) collective-permute-start(s32[96]{0:T(128)S(1)} %add_bitcast_fusion.col_a), channel_id=1, source_target_pairs={{0,4},{4,0},{8,12},{12,8},{16,20},{20,16},{24,28},{28,24},{32,36},... | collective-permute-start | bytes 1160 | tf_op jit(solution)/shard_map/ppermute | solution.py:39
  16.5 11.0 %copy-start.7 = (bf16[512,128]{1,0:T(8,128)(2,1)S(1)}, bf16[512,128]{1,0:T(8,128)(2,1)}, u32[]{:S(2)}) copy-start(bf16[512,128]{1,0:T(8,128)(2,1)} %param.7) | copy-start | bytes 393220
  25.0 26.5 %collective-permute-start.30 = (bf16[16,128,128]{2,1,0:T(8,128)(2,1)S(1)}, bf16[16,128,128]{2,1,0:T(8,128)(2,1)S(1)}, u32[]{:S(2)}, u32[]{:S(2)}) collective-permute-start(bf16[16,128,128]{2,1,0:T(8,128)(2,1)S(1)} %get-tuple-element.46), channel_id=1, source_target_pairs={{0,64},{4,68},{8,72},{12,76},{16,80},{20,84},{24,88},{28,92},{32,9... | collective-permute-start | bytes 1572872 | tf_op jit(solution)/shard_map/ppermute | solution.py:39
  26.6 24.9 %collective-permute-start.31 = (bf16[16,128,128]{2,1,0:T(8,128)(2,1)S(1)}, bf16[16,128,128]{2,1,0:T(8,128)(2,1)S(1)}, u32[]{:S(2)}, u32[]{:S(2)}) collective-permute-start(bf16[16,128,128]{2,1,0:T(8,128)(2,1)S(1)} %get-tuple-element.45), channel_id=1, source_target_pairs={{0,192},{4,196},{8,200},{12,204},{16,208},{20,212},{24,216},{28,22... | collective-permute-start | bytes 1572872 | tf_op jit(solution)/shard_map/ppermute | solution.py:39
  27.4 15.9 %collective-permute-start.2 = (bf16[4,128,128]{2,1,0:T(8,128)(2,1)S(1)}, bf16[4,128,128]{2,1,0:T(8,128)(2,1)S(1)}, u32[]{:S(2)}, u32[]{:S(2)}) collective-permute-start(bf16[4,128,128]{2,1,0:T(8,128)(2,1)S(1)} %bitcast.33), channel_id=1, source_target_pairs={{0,192},{4,196},{8,200},{12,204},{16,208},{20,212},{24,216},{28,22... | collective-permute-start | bytes 393224 | tf_op jit(solution)/shard_map/ppermute | solution.py:39
  30.6 15.3 %collective-permute-start.3 = (bf16[4,128,128]{2,1,0:T(8,128)(2,1)S(1)}, bf16[4,128,128]{2,1,0:T(8,128)(2,1)S(1)}, u32[]{:S(2)}, u32[]{:S(2)}) collective-permute-start(bf16[4,128,128]{2,1,0:T(8,128)(2,1)S(1)} %bitcast.34), channel_id=1, source_target_pairs={{0,128},{4,132},{8,136},{12,140},{16,144},{20,148},{24,152},{28,15... | collective-permute-start | bytes 393224 | tf_op jit(solution)/shard_map/ppermute | solution.py:39
  30.6 15.3 %collective-permute-start.4 = (bf16[4,128,128]{2,1,0:T(8,128)(2,1)S(1)}, bf16[4,128,128]{2,1,0:T(8,128)(2,1)S(1)}, u32[]{:S(2)}, u32[]{:S(2)}) collective-permute-start(bf16[4,128,128]{2,1,0:T(8,128)(2,1)S(1)} %bitcast.35), channel_id=1, source_target_pairs={{0,64},{4,68},{8,72},{12,76},{16,80},{20,84},{24,88},{28,92},{32,9... | collective-permute-start | bytes 393224 | tf_op jit(solution)/shard_map/ppermute | solution.py:39
  45.9 31.4 %copy-start.1 = (bf16[16,128,128]{2,1,0:T(8,128)(2,1)}, bf16[16,128,128]{2,1,0:T(8,128)(2,1)S(1)}, u32[]{:S(2)}) copy-start(bf16[16,128,128]{2,1,0:T(8,128)(2,1)S(1)} %join.2.rest_0_) | copy-start | bytes 1572868
  45.9 15.4 %collective-permute-start.8 = (bf16[16,128,128]{2,1,0:T(8,128)(2,1)S(1)}, bf16[16,128,128]{2,1,0:T(8,128)(2,1)S(1)}, u32[]{:S(2)}, u32[]{:S(2)}) collective-permute-start(bf16[16,128,128]{2,1,0:T(8,128)(2,1)S(1)} %join.2.rest_0_), channel_id=1, source_target_pairs={{0,8},{4,12},{8,16},{12,20},{16,24},{20,28},{24,32},{28,36},{32,40... | collective-permute-start | bytes 1572872 | tf_op jit(solution)/shard_map/ppermute | solution.py:39
  47.9 13.4 %collective-permute-start.5 = (bf16[16,128,128]{2,1,0:T(8,128)(2,1)S(1)}, bf16[16,128,128]{2,1,0:T(8,128)(2,1)S(1)}, u32[]{:S(2)}, u32[]{:S(2)}) collective-permute-start(bf16[16,128,128]{2,1,0:T(8,128)(2,1)S(1)} %join.2.rest_0_), channel_id=1, source_target_pairs={{0,56},{4,60},{8,0},{12,4},{16,8},{20,12},{24,16},{28,20},{32,24},... | collective-permute-start | bytes 1572872 | tf_op jit(solution)/shard_map/ppermute | solution.py:39
  51.8 25.0 %collective-permute-start.32 = (bf16[32,128,128]{2,1,0:T(8,128)(2,1)S(1)}, bf16[32,128,128]{2,1,0:T(8,128)(2,1)S(1)}, u32[]{:S(2)}, u32[]{:S(2)}) collective-permute-start(bf16[32,128,128]{2,1,0:T(8,128)(2,1)S(1)} %get-tuple-element.39), channel_id=1, source_target_pairs={{0,64},{4,68},{8,72},{12,76},{16,80},{20,84},{24,88},{28,92},{32,9... | collective-permute-start | bytes 3145736 | tf_op jit(solution)/shard_map/ppermute | solution.py:39
  51.9 24.9 %collective-permute-start.33 = (bf16[32,128,128]{2,1,0:T(8,128)(2,1)S(1)}, bf16[32,128,128]{2,1,0:T(8,128)(2,1)S(1)}, u32[]{:S(2)}, u32[]{:S(2)}) collective-permute-start(bf16[32,128,128]{2,1,0:T(8,128)(2,1)S(1)} %get-tuple-element.40), channel_id=1, source_target_pairs={{0,192},{4,196},{8,200},{12,204},{16,208},{20,212},{24,216},{28,22... | collective-permute-start | bytes 3145736 | tf_op jit(solution)/shard_map/ppermute | solution.py:39
  61.3 29.3 %copy-start.18 = (bf16[16,128,128]{2,1,0:T(8,128)(2,1)}, bf16[16,128,128]{2,1,0:T(8,128)(2,1)S(1)}, u32[]{:S(2)}) copy-start(bf16[16,128,128]{2,1,0:T(8,128)(2,1)S(1)} %collective-permute-done.8.rest_6_) | copy-start | bytes 1572868
  61.3 12.3 %collective-permute-start.9 = (bf16[16,128,128]{2,1,0:T(8,128)(2,1)S(1)}, bf16[16,128,128]{2,1,0:T(8,128)(2,1)S(1)}, u32[]{:S(2)}, u32[]{:S(2)}) collective-permute-start(bf16[16,128,128]{2,1,0:T(8,128)(2,1)S(1)} %collective-permute-done.8.rest_6_), channel_id=1, source_target_pairs={{0,8},{4,12},{8,16},{12,20},{16,24},{20,28},{24,32},{28,36},{32,40... | collective-permute-start | bytes 1572872 | tf_op jit(solution)/shard_map/ppermute | solution.py:39
  61.3 29.3 %copy-start.19 = (bf16[16,128,128]{2,1,0:T(8,128)(2,1)}, bf16[16,128,128]{2,1,0:T(8,128)(2,1)S(1)}, u32[]{:S(2)}) copy-start(bf16[16,128,128]{2,1,0:T(8,128)(2,1)S(1)} %collective-permute-done.5.rest_1_) | copy-start | bytes 1572868
  61.3 12.3 %collective-permute-start.6 = (bf16[16,128,128]{2,1,0:T(8,128)(2,1)S(1)}, bf16[16,128,128]{2,1,0:T(8,128)(2,1)S(1)}, u32[]{:S(2)}, u32[]{:S(2)}) collective-permute-start(bf16[16,128,128]{2,1,0:T(8,128)(2,1)S(1)} %collective-permute-done.5.rest_1_), channel_id=1, source_target_pairs={{0,56},{4,60},{8,0},{12,4},{16,8},{20,12},{24,16},{28,20},{32,24},... | collective-permute-start | bytes 1572872 | tf_op jit(solution)/shard_map/ppermute | solution.py:39
  73.6 17.0 %copy-start.20 = (bf16[16,128,128]{2,1,0:T(8,128)(2,1)}, bf16[16,128,128]{2,1,0:T(8,128)(2,1)S(1)}, u32[]{:S(2)}) copy-start(bf16[16,128,128]{2,1,0:T(8,128)(2,1)S(1)} %collective-permute-done.9.rest_5_) | copy-start | bytes 1572868
  73.6 12.3 %collective-permute-start.10 = (bf16[16,128,128]{2,1,0:T(8,128)(2,1)S(1)}, bf16[16,128,128]{2,1,0:T(8,128)(2,1)S(1)}, u32[]{:S(2)}, u32[]{:S(2)}) collective-permute-start(bf16[16,128,128]{2,1,0:T(8,128)(2,1)S(1)} %collective-permute-done.9.rest_5_), channel_id=1, source_target_pairs={{0,8},{4,12},{8,16},{12,20},{16,24},{20,28},{24,32},{28,36},{32,40... | collective-permute-start | bytes 1572872 | tf_op jit(solution)/shard_map/ppermute | solution.py:39
  73.6 17.0 %copy-start.21 = (bf16[16,128,128]{2,1,0:T(8,128)(2,1)}, bf16[16,128,128]{2,1,0:T(8,128)(2,1)S(1)}, u32[]{:S(2)}) copy-start(bf16[16,128,128]{2,1,0:T(8,128)(2,1)S(1)} %collective-permute-done.6.rest_2_) | copy-start | bytes 1572868
  73.6 15.1 %collective-permute-start.7 = (bf16[16,128,128]{2,1,0:T(8,128)(2,1)S(1)}, bf16[16,128,128]{2,1,0:T(8,128)(2,1)S(1)}, u32[]{:S(2)}, u32[]{:S(2)}) collective-permute-start(bf16[16,128,128]{2,1,0:T(8,128)(2,1)S(1)} %collective-permute-done.6.rest_2_), channel_id=1, source_target_pairs={{0,56},{4,60},{8,0},{12,4},{16,8},{20,12},{24,16},{28,20},{32,24},... | collective-permute-start | bytes 1572872 | tf_op jit(solution)/shard_map/ppermute | solution.py:39
  77.3 26.4 %collective-permute-start.34 = (bf16[16,128,128]{2,1,0:T(8,128)(2,1)S(1)}, bf16[16,128,128]{2,1,0:T(8,128)(2,1)S(1)}, u32[]{:S(2)}, u32[]{:S(2)}) collective-permute-start(bf16[16,128,128]{2,1,0:T(8,128)(2,1)S(1)} %get-tuple-element.42), channel_id=1, source_target_pairs={{0,8},{4,12},{8,0},{12,4},{16,24},{20,28},{24,16},{28,20},{32,40},... | collective-permute-start | bytes 1572872 | tf_op jit(solution)/shard_map/ppermute | solution.py:153
  85.9 12.5 %collective-permute-start.11 = (bf16[8,128,128]{2,1,0:T(8,128)(2,1)S(1)}, bf16[8,128,128]{2,1,0:T(8,128)(2,1)S(1)}, u32[]{:S(2)}, u32[]{:S(2)}) collective-permute-start(bf16[8,128,128]{2,1,0:T(8,128)(2,1)S(1)} %slice.62), channel_id=1, source_target_pairs={{0,8},{4,12},{8,16},{12,20},{16,24},{20,28},{24,32},{28,36},{32,40... | collective-permute-start | bytes 786440 | tf_op jit(solution)/shard_map/ppermute | solution.py:39
  88.7 12.2 %collective-permute-start.12 = (bf16[8,128,128]{2,1,0:T(8,128)(2,1)S(1)}, bf16[8,128,128]{2,1,0:T(8,128)(2,1)S(1)}, u32[]{:S(2)}, u32[]{:S(2)}) collective-permute-start(bf16[8,128,128]{2,1,0:T(8,128)(2,1)S(1)} %slice.63), channel_id=1, source_target_pairs={{0,56},{4,60},{8,0},{12,4},{16,8},{20,12},{24,16},{28,20},{32,24},... | collective-permute-start | bytes 786440 | tf_op jit(solution)/shard_map/ppermute | solution.py:39
  103.5 8.0 %copy-start.2 = (bf16[512,512]{1,0:T(8,128)(2,1)S(1)}, bf16[512,512]{1,0:T(8,128)(2,1)}, u32[]{:S(2)}) copy-start(bf16[512,512]{1,0:T(8,128)(2,1)} %w_two.1) | copy-start | bytes 1572868
  103.5 16.1 %copy-start.3 = (bf16[512,512]{1,0:T(8,128)(2,1)S(1)}, bf16[512,512]{1,0:T(8,128)(2,1)}, u32[]{:S(2)}) copy-start(bf16[512,512]{1,0:T(8,128)(2,1)} %w_in.1) | copy-start | bytes 1572868
  103.5 16.1 %copy-start.8 = (s32[4]{0:T(128)S(1)}, s32[4]{0:T(128)}, u32[]{:S(2)}) copy-start(s32[4]{0:T(128)} %pad_add_fusion.place) | copy-start | bytes 52
  103.5 3.3 %collective-permute-start.13 = (f32[4,128,128]{2,1,0:T(8,128)S(1)}, f32[4,128,128]{2,1,0:T(8,128)S(1)}, u32[]{:S(2)}, u32[]{:S(2)}) collective-permute-start(f32[4,128,128]{2,1,0:T(8,128)S(1)} %get-tuple-element.27), channel_id=1, source_target_pairs={{0,4},{4,0},{8,12},{12,8},{16,20},{20,16},{24,28},{28,24},{32,36},... | collective-permute-start | bytes 786440 | tf_op jit(solution)/shard_map/ppermute | solution.py:39
  103.8 20.9 %collective-permute-start.35 = (bf16[8,128,128]{2,1,0:T(8,128)(2,1)S(1)}, bf16[8,128,128]{2,1,0:T(8,128)(2,1)S(1)}, u32[]{:S(2)}, u32[]{:S(2)}) collective-permute-start(bf16[8,128,128]{2,1,0:T(8,128)(2,1)S(1)} %slice.86), channel_id=1, source_target_pairs={{0,16},{4,20},{8,24},{12,28},{16,0},{20,4},{24,8},{28,12},{32,48},... | collective-permute-start | bytes 786440 | tf_op jit(solution)/shard_map/ppermute | solution.py:157
  106.8 9.0 %collective-permute-start.14 = (bf16[512,128]{1,0:T(8,128)(2,1)S(1)}, bf16[512,128]{1,0:T(8,128)(2,1)S(1)}, u32[]{:S(2)}, u32[]{:S(2)}) collective-permute-start(bf16[512,128]{1,0:T(8,128)(2,1)S(1)} %bitcast.24), channel_id=1, source_target_pairs={{0,3},{1,0},{2,1},{3,2},{4,7},{5,4},{6,5},{7,6},{8,11},{9,8},{10,9... | collective-permute-start | bytes 393224 | tf_op jit(solution)/shard_map/ppermute | solution.py:44
  109.9 7.9 %collective-permute-start.15 = (bf16[512,128]{1,0:T(8,128)(2,1)S(1)}, bf16[512,128]{1,0:T(8,128)(2,1)S(1)}, u32[]{:S(2)}, u32[]{:S(2)}) collective-permute-start(bf16[512,128]{1,0:T(8,128)(2,1)S(1)} %bitcast.25), channel_id=1, source_target_pairs={{0,2},{1,3},{2,0},{3,1},{4,6},{5,7},{6,4},{7,5},{8,10},{9,11},{10,... | collective-permute-start | bytes 393224 | tf_op jit(solution)/shard_map/ppermute | solution.py:44
  110.6 9.0 %collective-permute-start.16 = (bf16[512,128]{1,0:T(8,128)(2,1)S(1)}, bf16[512,128]{1,0:T(8,128)(2,1)S(1)}, u32[]{:S(2)}, u32[]{:S(2)}) collective-permute-start(bf16[512,128]{1,0:T(8,128)(2,1)S(1)} %bitcast.26), channel_id=1, source_target_pairs={{0,1},{1,2},{2,3},{3,0},{4,5},{5,6},{6,7},{7,4},{8,9},{9,10},{10,1... | collective-permute-start | bytes 393224 | tf_op jit(solution)/shard_map/ppermute | solution.py:44
  121.9 7.6 %collective-permute-start.17 = (bf16[4,128,128]{2,1,0:T(8,128)(2,1)S(1)}, bf16[4,128,128]{2,1,0:T(8,128)(2,1)S(1)}, u32[]{:S(2)}, u32[]{:S(2)}) collective-permute-start(bf16[4,128,128]{2,1,0:T(8,128)(2,1)S(1)} %get-tuple-element.28.refs_0_), channel_id=1, source_target_pairs={{0,192},{4,196},{8,200},{12,204},{16,208},{20,212},{24,216},{28,22... | collective-permute-start | bytes 393224 | tf_op jit(solution)/shard_map/ppermute | solution.py:39
  122.0 8.9 %collective-permute-start.18 = (bf16[4,128,128]{2,1,0:T(8,128)(2,1)S(1)}, bf16[4,128,128]{2,1,0:T(8,128)(2,1)S(1)}, u32[]{:S(2)}, u32[]{:S(2)}) collective-permute-start(bf16[4,128,128]{2,1,0:T(8,128)(2,1)S(1)} %get-tuple-element.28.refs_0_), channel_id=1, source_target_pairs={{0,128},{4,132},{8,136},{12,140},{16,144},{20,148},{24,152},{28,15... | collective-permute-start | bytes 393224 | tf_op jit(solution)/shard_map/ppermute | solution.py:39
  124.7 7.3 %collective-permute-start.19 = (bf16[4,128,128]{2,1,0:T(8,128)(2,1)S(1)}, bf16[4,128,128]{2,1,0:T(8,128)(2,1)S(1)}, u32[]{:S(2)}, u32[]{:S(2)}) collective-permute-start(bf16[4,128,128]{2,1,0:T(8,128)(2,1)S(1)} %get-tuple-element.28.refs_0_), channel_id=1, source_target_pairs={{0,64},{4,68},{8,72},{12,76},{16,80},{20,84},{24,88},{28,92},{32,9... | collective-permute-start | bytes 393224 | tf_op jit(solution)/shard_map/ppermute | solution.py:39
  125.8 9.8 %collective-permute-start.36 = (bf16[4,128,128]{2,1,0:T(8,128)(2,1)S(1)}, bf16[4,128,128]{2,1,0:T(8,128)(2,1)S(1)}, u32[]{:S(2)}, u32[]{:S(2)}) collective-permute-start(bf16[4,128,128]{2,1,0:T(8,128)(2,1)S(1)} %slice.87), channel_id=1, source_target_pairs={{0,32},{4,36},{8,40},{12,44},{16,48},{20,52},{24,56},{28,60},{32,0... | collective-permute-start | bytes 393224 | tf_op jit(solution)/shard_map/ppermute | solution.py:157
  132.0 51.8 %copy-start = (bf16[16,128,128]{2,1,0:T(8,128)(2,1)}, bf16[16,128,128]{2,1,0:T(8,128)(2,1)S(1)}, u32[]{:S(2)}) copy-start(bf16[16,128,128]{2,1,0:T(8,128)(2,1)S(1)} %join.3.rest_0_) | copy-start | bytes 1572868
  132.1 17.2 %collective-permute-start.20 = (bf16[16,128,128]{2,1,0:T(8,128)(2,1)S(1)}, bf16[16,128,128]{2,1,0:T(8,128)(2,1)S(1)}, u32[]{:S(2)}, u32[]{:S(2)}) collective-permute-start(bf16[16,128,128]{2,1,0:T(8,128)(2,1)S(1)} %join.3.rest_0_), channel_id=1, source_target_pairs={{0,56},{4,60},{8,0},{12,4},{16,8},{20,12},{24,16},{28,20},{32,24},... | collective-permute-start | bytes 1572872 | tf_op jit(solution)/shard_map/ppermute | solution.py:39
  132.3 19.0 %collective-permute-start.23 = (bf16[16,128,128]{2,1,0:T(8,128)(2,1)S(1)}, bf16[16,128,128]{2,1,0:T(8,128)(2,1)}, u32[]{:S(2)}, u32[]{:S(2)}) collective-permute-start(bf16[16,128,128]{2,1,0:T(8,128)(2,1)S(1)} %join.3.rest_0_), channel_id=1, source_target_pairs={{0,8},{4,12},{8,16},{12,20},{16,24},{20,28},{24,32},{28,36},{32,40... | collective-permute-start | bytes 1572872 | tf_op jit(solution)/shard_map/ppermute | solution.py:39
  135.8 6.5 %collective-permute-start.37 = (bf16[512,128]{1,0:T(8,128)(2,1)S(1)}, bf16[512,128]{1,0:T(8,128)(2,1)S(1)}, u32[]{:S(2)}, u32[]{:S(2)}) collective-permute-start(bf16[512,128]{1,0:T(8,128)(2,1)S(1)} %bitcast.29), channel_id=1, source_target_pairs={{0,3},{1,0},{2,1},{3,2},{4,7},{5,4},{6,5},{7,6},{8,11},{9,8},{10,9... | collective-permute-start | bytes 393224 | tf_op jit(solution)/shard_map/ppermute | solution.py:44
  138.4 6.6 %collective-permute-start.38 = (bf16[512,128]{1,0:T(8,128)(2,1)S(1)}, bf16[512,128]{1,0:T(8,128)(2,1)S(1)}, u32[]{:S(2)}, u32[]{:S(2)}) collective-permute-start(bf16[512,128]{1,0:T(8,128)(2,1)S(1)} %bitcast.30), channel_id=1, source_target_pairs={{0,2},{1,3},{2,0},{3,1},{4,6},{5,7},{6,4},{7,5},{8,10},{9,11},{10,... | collective-permute-start | bytes 393224 | tf_op jit(solution)/shard_map/ppermute | solution.py:44
  139.0 7.3 %collective-permute-start.39 = (bf16[512,128]{1,0:T(8,128)(2,1)S(1)}, bf16[512,128]{1,0:T(8,128)(2,1)S(1)}, u32[]{:S(2)}, u32[]{:S(2)}) collective-permute-start(bf16[512,128]{1,0:T(8,128)(2,1)S(1)} %bitcast.31), channel_id=1, source_target_pairs={{0,1},{1,2},{2,3},{3,0},{4,5},{5,6},{6,7},{7,4},{8,9},{9,10},{10,1... | collective-permute-start | bytes 393224 | tf_op jit(solution)/shard_map/ppermute | solution.py:44
  146.3 55.1 %copy-start.5 = (s32[1232]{0:T(1024)S(1)}, s32[1232]{0:T(1024)}, u32[]{:S(2)}) copy-start(s32[1232]{0:T(1024)} %plan.1.lists) | copy-start | bytes 14788
  149.1 2.2 %collective-permute-start.40 = (f32[512,128]{1,0:T(8,128)S(1)}, f32[512,128]{1,0:T(8,128)S(1)}, u32[]{:S(2)}, u32[]{:S(2)}) collective-permute-start(f32[512,128]{1,0:T(8,128)S(1)} %get-tuple-element.44), channel_id=1, source_target_pairs={{0,4},{4,0},{8,12},{12,8},{16,20},{20,16},{24,28},{28,24},{32,36},... | collective-permute-start | bytes 786440 | tf_op jit(solution)/shard_map/ppermute | solution.py:163
  149.2 52.2 %copy-start.15 = (bf16[16,128,128]{2,1,0:T(8,128)(2,1)}, bf16[16,128,128]{2,1,0:T(8,128)(2,1)S(1)}, u32[]{:S(2)}) copy-start(bf16[16,128,128]{2,1,0:T(8,128)(2,1)S(1)} %collective-permute-done.20.rest_1_) | copy-start | bytes 1572868
  149.3 14.3 %collective-permute-start.21 = (bf16[16,128,128]{2,1,0:T(8,128)(2,1)S(1)}, bf16[16,128,128]{2,1,0:T(8,128)(2,1)S(1)}, u32[]{:S(2)}, u32[]{:S(2)}) collective-permute-start(bf16[16,128,128]{2,1,0:T(8,128)(2,1)S(1)} %collective-permute-done.20.rest_1_), channel_id=1, source_target_pairs={{0,56},{4,60},{8,0},{12,4},{16,8},{20,12},{24,16},{28,20},{32,24},... | collective-permute-start | bytes 1572872 | tf_op jit(solution)/shard_map/ppermute | solution.py:39
  151.4 15.4 %collective-permute-start.24 = (bf16[16,128,128]{2,1,0:T(8,128)(2,1)}, bf16[16,128,128]{2,1,0:T(8,128)(2,1)S(1)}, u32[]{:S(2)}, u32[]{:S(2)}) collective-permute-start(bf16[16,128,128]{2,1,0:T(8,128)(2,1)} %collective-permute-done.23.rest_6_), channel_id=1, source_target_pairs={{0,8},{4,12},{8,16},{12,20},{16,24},{20,28},{24,32},{28,36},{32,40... | collective-permute-start | bytes 1572872 | tf_op jit(solution)/shard_map/ppermute | solution.py:39
  151.4 15.4 %collective-permute-start.41 = (f32[256,128]{1,0:T(8,128)S(1)}, f32[256,128]{1,0:T(8,128)S(1)}, u32[]{:S(2)}, u32[]{:S(2)}) collective-permute-start(f32[256,128]{1,0:T(8,128)S(1)} %slice_select_fusion), channel_id=1, source_target_pairs={{0,64},{4,68},{8,72},{12,76},{16,80},{20,84},{24,88},{28,92},{32,9... | collective-permute-start | bytes 393224 | tf_op jit(solution)/shard_map/ppermute | solution.py:169
  163.6 37.9 %copy-start.16 = (bf16[16,128,128]{2,1,0:T(8,128)(2,1)}, bf16[16,128,128]{2,1,0:T(8,128)(2,1)S(1)}, u32[]{:S(2)}) copy-start(bf16[16,128,128]{2,1,0:T(8,128)(2,1)S(1)} %collective-permute-done.21.rest_2_) | copy-start | bytes 1572868
  163.6 20.3 %collective-permute-start.22 = (bf16[16,128,128]{2,1,0:T(8,128)(2,1)S(1)}, bf16[16,128,128]{2,1,0:T(8,128)(2,1)S(1)}, u32[]{:S(2)}, u32[]{:S(2)}) collective-permute-start(bf16[16,128,128]{2,1,0:T(8,128)(2,1)S(1)} %collective-permute-done.21.rest_2_), channel_id=1, source_target_pairs={{0,56},{4,60},{8,0},{12,4},{16,8},{20,12},{24,16},{28,20},{32,24},... | collective-permute-start | bytes 1572872 | tf_op jit(solution)/shard_map/ppermute | solution.py:39
  166.8 34.6 %copy-start.17 = (bf16[16,128,128]{2,1,0:T(8,128)(2,1)}, bf16[16,128,128]{2,1,0:T(8,128)(2,1)S(1)}, u32[]{:S(2)}) copy-start(bf16[16,128,128]{2,1,0:T(8,128)(2,1)S(1)} %collective-permute-done.24.rest_5_) | copy-start | bytes 1572868
  166.8 14.4 %collective-permute-start.25 = (bf16[16,128,128]{2,1,0:T(8,128)(2,1)S(1)}, bf16[16,128,128]{2,1,0:T(8,128)(2,1)S(1)}, u32[]{:S(2)}, u32[]{:S(2)}) collective-permute-start(bf16[16,128,128]{2,1,0:T(8,128)(2,1)S(1)} %collective-permute-done.24.rest_5_), channel_id=1, source_target_pairs={{0,8},{4,12},{8,16},{12,20},{16,24},{20,28},{24,32},{28,36},{32,40... | collective-permute-start | bytes 1572872 | tf_op jit(solution)/shard_map/ppermute | solution.py:39
  166.8 6.6 %collective-permute-start.42 = (f32[256,128]{1,0:T(8,128)S(1)}, f32[256,128]{1,0:T(8,128)S(1)}, u32[]{:S(2)}, u32[]{:S(2)}) collective-permute-start(f32[256,128]{1,0:T(8,128)S(1)} %select_add_fusion), channel_id=1, source_target_pairs={{0,128},{4,132},{8,136},{12,140},{16,144},{20,148},{24,152},{28,15... | collective-permute-start | bytes 393224 | tf_op jit(solution)/shard_map/ppermute | solution.py:171
  173.4 7.7 %collective-permute-start.43 = (f32[256,128]{1,0:T(8,128)S(1)}, f32[256,128]{1,0:T(8,128)S(1)}, u32[]{:S(2)}, u32[]{:S(2)}) collective-permute-start(f32[256,128]{1,0:T(8,128)S(1)} %add.59), channel_id=1, source_target_pairs={{0,8},{4,12},{8,0},{12,4},{16,24},{20,28},{24,16},{28,20},{32,40},... | collective-permute-start | bytes 393224 | tf_op jit(solution)/shard_map/ppermute | solution.py:171
  181.1 9.2 %collective-permute-start.44 = (f32[256,128]{1,0:T(8,128)S(1)}, f32[256,128]{1,0:T(8,128)S(1)}, u32[]{:S(2)}, u32[]{:S(2)}) collective-permute-start(f32[256,128]{1,0:T(8,128)S(1)} %add.60), channel_id=1, source_target_pairs={{0,16},{4,20},{8,24},{12,28},{16,0},{20,4},{24,8},{28,12},{32,48},... | collective-permute-start | bytes 393224 | tf_op jit(solution)/shard_map/ppermute | solution.py:171
  181.2 20.2 %copy-start.12 = (bf16[16,128,128]{2,1,0:T(8,128)(2,1)}, bf16[16,128,128]{2,1,0:T(8,128)(2,1)S(1)}, u32[]{:S(2)}) copy-start(bf16[16,128,128]{2,1,0:T(8,128)(2,1)S(1)} %collective-permute-done.25.rest_4_) | copy-start | bytes 1572868
  181.3 27.6 %collective-permute-start.26 = (bf16[8,128,128]{2,1,0:T(8,128)(2,1)S(1)}, bf16[8,128,128]{2,1,0:T(8,128)(2,1)S(1)}, u32[]{:S(2)}, u32[]{:S(2)}) collective-permute-start(bf16[8,128,128]{2,1,0:T(8,128)(2,1)S(1)} %slice.64), channel_id=1, source_target_pairs={{0,8},{4,12},{8,16},{12,20},{16,24},{20,28},{24,32},{28,36},{32,40... | collective-permute-start | bytes 786440 | tf_op jit(solution)/shard_map/ppermute | solution.py:39
  183.8 17.6 %copy-start.11 = (bf16[16,128,128]{2,1,0:T(8,128)(2,1)}, bf16[16,128,128]{2,1,0:T(8,128)(2,1)S(1)}, u32[]{:S(2)}) copy-start(bf16[16,128,128]{2,1,0:T(8,128)(2,1)S(1)} %collective-permute-done.22.rest_3_) | copy-start | bytes 1572868
  183.9 25.0 %collective-permute-start.27 = (bf16[8,128,128]{2,1,0:T(8,128)(2,1)S(1)}, bf16[8,128,128]{2,1,0:T(8,128)(2,1)S(1)}, u32[]{:S(2)}, u32[]{:S(2)}) collective-permute-start(bf16[8,128,128]{2,1,0:T(8,128)(2,1)S(1)} %slice.65), channel_id=1, source_target_pairs={{0,56},{4,60},{8,0},{12,4},{16,8},{20,12},{24,16},{28,20},{32,24},... | collective-permute-start | bytes 786440 | tf_op jit(solution)/shard_map/ppermute | solution.py:39
  190.4 9.9 %collective-permute-start.45 = (f32[256,128]{1,0:T(8,128)S(1)}, f32[256,128]{1,0:T(8,128)S(1)}, u32[]{:S(2)}, u32[]{:S(2)}) collective-permute-start(f32[256,128]{1,0:T(8,128)S(1)} %add.61), channel_id=1, source_target_pairs={{0,32},{4,36},{8,40},{12,44},{16,48},{20,52},{24,56},{28,60},{32,0... | collective-permute-start | bytes 393224 | tf_op jit(solution)/shard_map/ppermute | solution.py:171
  200.2 11.3 %collective-permute-start.46 = (f32[256,128]{1,0:T(8,128)S(1)}, f32[256,128]{1,0:T(8,128)S(1)}, u32[]{:S(2)}, u32[]{:S(2)}) collective-permute-start(f32[256,128]{1,0:T(8,128)S(1)} %add.62), channel_id=1, source_target_pairs={{0,64},{4,68},{8,72},{12,76},{16,80},{20,84},{24,88},{28,92},{32,9... | collective-permute-start | bytes 393224 | tf_op jit(solution)/shard_map/ppermute | solution.py:178
  211.5 1.6 collective-permute-start.28
  211.6 2.1 collective-permute-start.47
  (8 other events, 21.5 us)
